TPU v7x, 256 devices: a whole 4x4x8 slice. The times are simulated.
256 devices in a mesh: row: 8 (over y, z_hi), col: 32 (over z_lo, x, core).
Axes of the slice: x: 4, y: 4, z: 8 (z_hi: 2, z_lo: 4; z = z_hi * 4 + z_lo), core: 2. Of those that a mesh axis runs over, the one named last changes fastest.
Arguments:
- p_values: bfloat16 [8192, 8192], P('row', 'col'), may hold values from -0.164701961 to 0.164701961, as said below
- occupancy: int32 [64, 64], replicated, may hold values from 0 to 1, as said below
- square_pattern: int32 [64, 64], replicated, may hold values 0 or 1
- cube_pattern: int32 [64, 64], replicated, may hold values 0 or 1
- block_order: int32 [64], replicated, may hold values from 0 to 63, each once
Outputs:
- purified: float32 [8192, 8192], P('row', 'col')
Inputs may be any that keep to these rules, and one draw needn't show every extreme that they name: p_values is symmetric. occupancy is 1 on the diagonal and on the 8 diagonals above it, 0 below the diagonal and beyond 3 * (8) diagonals above it, and 0 or 1 in between.
All inputs are finite; a program needn't handle non-finite values.
Results may differ from a plain program's by a relative error of at most 0.0016.
Values may be sent and summed in bfloat16 or wider, within the bound.
A program may use at most 128 MiB of HBM per device.

v0:
```python
import jax
import jax.numpy as jnp
from jax import lax
from jax.sharding import Mesh
from jax.sharding import PartitionSpec as P

ROW = ("row_0", "row_1")


def gathered_by_axis(array, axes, dim):
    filled = array
    for number in range(len(axes) - 1, -1, -1):
        filled = lax.all_gather(filled, axes[number], axis=dim, tiled=True)
    return filled


def mirrored(upper_part):
    upper_only = jnp.triu(upper_part)
    return (upper_only + jnp.triu(upper_part, 1).T).astype(jnp.float32)


def selector(positions, block_width, block_order):
    block_count = block_order.shape[0]
    labels = jnp.arange(block_count, dtype=jnp.int32)
    stored_hot = ((positions // block_width)[:, None] == labels[None, :]).astype(jnp.float32)
    natural_hot = (block_order[:, None] == labels[None, :]).astype(jnp.float32)
    return jnp.dot(stored_hot, natural_hot, precision=lax.Precision.HIGHEST)


def tile_mask(upper_part, row_select, col_select):
    inner = jnp.dot(row_select, mirrored(upper_part), precision=lax.Precision.HIGHEST)
    return jnp.dot(inner, col_select.T, precision=lax.Precision.HIGHEST) > 0.5


def body(p_values, occupancy, square_pattern, cube_pattern, block_order):
    local_rows, local_cols = p_values.shape
    matrix_order = local_cols * lax.axis_size("col")
    block_width = matrix_order // occupancy.shape[0]
    row_positions = lax.axis_index(ROW) * local_rows + jnp.arange(local_rows, dtype=jnp.int32)
    col_positions = lax.axis_index("col") * local_cols + jnp.arange(local_cols, dtype=jnp.int32)
    row_select = selector(row_positions, block_width, block_order)
    col_select = selector(col_positions, block_width, block_order)
    keep_p = tile_mask(occupancy, row_select, col_select)
    keep_square = tile_mask(square_pattern, row_select, col_select)
    keep_cube = tile_mask(cube_pattern, row_select, col_select)
    p_tile = jnp.where(keep_p, p_values, jnp.zeros_like(p_values))
    p_panel = lax.all_gather(p_tile, "col", axis=1, tiled=True)

    def panel_step(shard_piece):
        return jnp.dot(p_panel, shard_piece, preferred_element_type=jnp.float32)

    squared = panel_step(lax.all_gather(p_tile, ROW, axis=0, tiled=True))
    squared = jnp.where(keep_square, squared, jnp.zeros_like(squared))
    square_half = squared.astype(jnp.bfloat16)
    cubed = panel_step(gathered_by_axis(square_half, ROW, 0))
    cubed = jnp.where(keep_cube, cubed, jnp.zeros_like(cubed))
    return 3.0 * squared - 2.0 * cubed


def solution(mesh):
    finer = Mesh(mesh.devices.reshape(4, 2, mesh.shape["col"]), ("row_0", "row_1", "col"))
    placed = (P(ROW, "col"), P(), P(), P(), P())
    return jax.shard_map(
        body, mesh=finer, in_specs=placed, out_specs=P(ROW, "col"), check_vma=False
    )
```

profile of v0, /device:TPU:1, one launch (start us, length us, event | category | flops | bytes accessed | tf_op | source)
XLA Modules:
  0.0 365.3 jit_solution(16066008766939892894)
XLA Ops:
  6.6 0.8 copy.9
  7.4 0.9 fusion.5
  8.3 1.0 fusion.3
  9.4 1.8 fusion.11
  11.2 2.8 fusion.2
  14.0 0.0 all-gather.5.cloned.1.call-start
  14.1 0.7 all-gather.5.cloned.1.call-update
  14.8 0.0 all-gather.9.cloned.1.call-start
  14.8 0.8 copy.7
  15.6 1.8 fusion.14
  17.4 1.0 convolution_compare_fusion.2
  18.4 106.2 %all-gather.7.cloned.1.call-done = bf16[8192,256]{1,0:T(8,128)(2,1)} async-done(((bf16[1024,256]{1,0:T(8,128)(2,1)}), bf16[8192,256]{1,0:T(8,128)(2,1)}) %all-gather.7.cloned.1.call-update) | async-done | bytes 4194320 | tf_op jit(solution)/shard_map/all_gather | solution.py:52
  124.6 120.7 %all-gather.5.cloned.1.call-done = bf16[1024,8192]{1,0:T(8,128)(2,1)} async-done(((bf16[1024,256]{1,0:T(8,128)(2,1)}), bf16[1024,8192]{1,0:T(8,128)(2,1)}) %all-gather.5.cloned.1.call-update) | async-done | bytes 16777232 | tf_op jit(solution)/shard_map/all_gather | solution.py:47
  245.3 12.2 %fusion.38 = (bf16[1024,256]{1,0:T(8,128)(2,1)}, f32[1024,256]{1,0:T(8,128)S(1)}) fusion(pred[1024,256]{1,0:T(32,128)(4,1)S(1)} %convolution_compare_fusion.2, bf16[1024,8192]{1,0:T(8,128)(2,1)} %all-gather.5.cloned.1.call-done, bf16[8192,256]{1,0:T(8,128)(2,1)} %all-gather.7.cloned.1.call-done), kind=kOutput, calls=%fused_computation.59 | convolution fusion | flops 4295491584 | bytes 22806528 | tf_op jit(solution)/shard_map/dot_general | solution.py:50
  257.6 0.2 all-gather.11.cloned.1.call-start
  257.8 39.7 %all-gather.9.cloned.1.call-done = bf16[2048,256]{1,0:T(8,128)(2,1)} async-done(((bf16[1024,256]{1,0:T(8,128)(2,1)}), bf16[2048,256]{1,0:T(8,128)(2,1)}) %all-gather.9.cloned.1.call-update) | async-done | bytes 1048592 | tf_op jit(solution)/shard_map/all_gather | solution.py:13
  297.5 0.1 iota_compare_fusion.5
  297.6 0.1 copy.10
  297.7 0.1 copy.12
  297.8 0.1 copy.11
  297.9 1.0 fusion.8
  298.9 1.0 convolution_compare_fusion
  299.8 46.5 %all-gather.11.cloned.1.call-done = bf16[8192,256]{1,0:T(8,128)(2,1)} async-done(((bf16[2048,256]{1,0:T(8,128)(2,1)}), bf16[8192,256]{1,0:T(8,128)(2,1)}) %all-gather.11.cloned.1.call-update) | async-done | bytes 4194320 | tf_op jit(solution)/shard_map/all_gather | solution.py:13
  346.3 12.4 %fusion.1 = f32[1024,256]{1,0:T(8,128)} fusion(pred[1024,256]{1,0:T(32,128)(4,1)S(1)} %convolution_compare_fusion, bf16[1024,8192]{1,0:T(8,128)(2,1)} %all-gather.5.cloned.1.call-done, bf16[8192,256]{1,0:T(8,128)(2,1)} %all-gather.11.cloned.1.call-done, f32[1024,256]{1,0:T(8,128)S(1)} %get-tuple-element.6), kind=kOutput, calls=%fused_computation.2 | convolution fusion | flops 4296015872 | bytes 23330816 | tf_op jit(solution)/shard_map/dot_general | solution.py:50
  (10 shorter events, 0.1 us)
Async XLA Ops:
  6.5 118.1 %all-gather.7.cloned.1.call-start = ((), (), s32[]{:S(2)}) async-start(), calls=%async_computation.1 | async-start | bytes 4718592 | tf_op jit(solution)/shard_map/all_gather | solution.py:52
  14.0 231.3 %all-gather.5.cloned.1.call-start = ((), (), s32[]{:S(2)}) async-start(), calls=%async_computation | async-start | bytes 17301504 | tf_op jit(solution)/shard_map/all_gather | solution.py:47
  14.8 282.7 %all-gather.9.cloned.1.call-start = ((), (), s32[]{:S(2)}) async-start(), calls=%async_computation.2 | async-start | bytes 1572864 | tf_op jit(solution)/shard_map/all_gather | solution.py:13
  18.4 279.4 %copy-start = (s32[64,64]{1,0:T(8,128)S(1)}, s32[64,64]{1,0:T(8,128)}, u32[]{:S(2)}) copy-start(s32[64,64]{1,0:T(8,128)} %param.8) | copy-start | bytes 49156
  257.6 88.8 %all-gather.11.cloned.1.call-start = ((), (), s32[]{:S(2)}) async-start(), calls=%async_computation.3 | async-start | bytes 5242880 | tf_op jit(solution)/shard_map/all_gather | solution.py:13
Sparse Core Ops, SparseCore 0:
  14.1 110.4 all-gather.6
  126.4 118.8 all-gather.4
  257.7 39.7 all-gather.8
  299.1 47.1 all-gather.10
where the time goes:
time: 366 us; the launch traced here: 365 us
  waiting for transfers between devices  314 us (86%)
  matrix products  36 us (10%)
  between operations  13.2 us (4%)
    all_gather x1, waiting for transfers between devices, body(): p_panel = lax.all_gather(p_tile, 'col', axis=1, tiled=True)  121 us
    all_gather x1, waiting for transfers between devices, body(): squared = panel_step(lax.all_gather(p_tile, ROW, axis=0, tiled=True))  106 us
    all_gather x2, waiting for transfers between devices, gathered_by_axis(): filled = lax.all_gather(filled, axes[number], axis=dim, tiled=True)  86.1 us
    dot_general x2, matrix products, panel_step(): return jnp.dot(p_panel, shard_piece, preferred_element_type=jnp.float32)  24.7 us
  transfers between devices with their start and end apart: 4, of which 4 were waited for; matrix products, arithmetic and copies ran while one was open for 2% of the time, Pallas kernels for 0%

commit v1 on v0

v1 whole, which is shorter than its diff:
```python
import functools
import jax
import jax.numpy as jnp
from jax import lax
from jax.experimental import pallas as pl
from jax.experimental.pallas import tpu as pltpu
from jax.sharding import Mesh
from jax.sharding import PartitionSpec as P

AXES = ("y", "zh", "zl", "x", "core")
CHUNKS = 4
ORDER = (
    ("X", 1, 0, 0), ("X", -1, 3, 0), ("Z", 0, 0), ("Y", 1, 0, 0, 3), ("Y", -1, 0, 0, 1), ("X", -1, 1, 0), ("Z", 1, 0),
    ("X", -1, 2, 0), ("X", 1, 1, 0), ("X", -1, 0, 0), ("Y", 1, 0, 0, 2), ("Z", 0, 1), ("Y", 1, 0, 0, 0), ("X", 1, 0, 1),
    ("X", 1, 2, 0), ("YF", 1, 0, 0, 2), ("Z", 2, 0), ("Y", -1, 0, 0, 0), ("Z", 0, 2), ("Y", 1, 0, 0, 1), ("XF", 1, 0, 1),
    ("X", 1, 0, 2), ("X", -1, 0, 1), ("X", -1, 0, 2), ("Z", 0, 3), ("YF", 1, 0, 0, 0), ("Y", -1, 0, 0, 3), ("X", 1, 3, 0),
    ("Z", 1, 1), ("X", -1, 0, 3), ("XF", 1, 0, 0), ("Z", 3, 0), ("XF", -1, 0, 2), ("Y", -1, 0, 0, 2), ("X", 1, 0, 3),
    ("Z", 1, 2), ("Z", 2, 1), ("YF", -1, 0, 0, 3), ("YF", -1, 0, 0, 1), ("XF", 1, 1, 0), ("XF", -1, 0, 3), ("SIB", 0, 0),
    ("Z", 1, 3), ("X", 1, 1, 1), ("X", -1, 1, 3), ("Y", 1, 0, 1, 0), ("X", -1, 1, 2), ("SIB", 1, 0), ("X", -1, 1, 1),
    ("X", 1, 1, 3), ("Z", 2, 2), ("SIB", 0, 2), ("Z", 3, 1), ("SIB", 0, -1), ("Y", -1, 0, 1, 0), ("SIB", 0, 1),
    ("X", 1, 1, 2), ("XF", -1, 1, 3), ("YF", 1, 0, 1, 0), ("Y", 1, 0, 1, 1), ("Z", 2, 3), ("Y", -1, 0, 1, 1), ("Z", 3, 2),
    ("SQ", 0, 0), ("XF", 1, 1, 1), ("XF", -1, 1, 2), ("YF", -1, 0, 1, 1), ("Z", 3, 3), ("SIB", 2, 0), ("Y", -1, 0, 1, 2),
    ("SIB", 1, -1), ("X", -1, 2, 3), ("X", 1, 2, 1), ("X", 1, 2, 3), ("Y", 1, 0, 1, 2), ("SIB", 1, 1), ("Y", -1, 0, 1, 3),
    ("SIB", 1, 2), ("Y", 1, 0, 1, 3), ("X", -1, 2, 2), ("X", -1, 2, 1), ("YF", 1, 0, 1, 2), ("SQ", 1, 0), ("X", 1, 2, 2),
    ("XF", 1, 2, 0), ("YF", -1, 0, 1, 3), ("XF", 1, 2, 1), ("XF", -1, 2, 2), ("XF", -1, 2, 3), ("SQ", 0, 1), ("ES", 0),
    ("Y", 1, 1, 0, 0), ("SQ", 1, 1), ("ES", 1), ("SIB", 2, -1), ("X", 1, 3, 3), ("SIB", 2, 1), ("Y", -1, 1, 0, 1),
    ("X", 1, 3, 1), ("SIB", 3, 0), ("X", -1, 3, 3), ("SIB", 2, 2), ("X", -1, 3, 1), ("Y", 1, 1, 0, 1), ("X", -1, 3, 2),
    ("YF", 1, 1, 0, 0), ("YF", -1, 1, 0, 1), ("X", 1, 3, 2), ("SQ", 2, 0), ("Y", 1, 1, 1, 0), ("SQ", 2, 1), ("ES", 2),
    ("Y", -1, 1, 0, 0), ("XF", -1, 3, 3), ("SIB", 3, -1), ("XF", 1, 3, 0), ("Y", -1, 1, 1, 1), ("Y", 1, 1, 0, 2),
    ("Y", -1, 1, 1, 0), ("XF", 1, 3, 1), ("XF", -1, 3, 2), ("YF", 1, 1, 1, 0), ("Y", 1, 1, 1, 2), ("Y", 1, 1, 1, 1),
    ("Y", -1, 1, 0, 2), ("SIB", 3, 1), ("SIB", 3, 2), ("YF", -1, 1, 1, 1), ("SQ", 3, 0), ("SQ", 3, 1), ("Y", -1, 1, 0, 3),
    ("CU", 0, 2, 0), ("Y", 1, 1, 0, 3), ("YF", 1, 1, 1, 2), ("YF", 1, 1, 0, 2), ("ES", 3), ("CU", 1, 2, 0), ("CU", 0, 0, 0),
    ("CU", 1, -1, 1), ("CU", 1, 0, 1), ("CU", 1, -1, 0), ("CU", 1, 2, 1), ("CU", 0, 2, 1), ("Y", -1, 1, 1, 2),
    ("CU", 0, 1, 2), ("CU", 0, 0, 1), ("YF", -1, 1, 0, 3), ("CU", 1, 1, 1), ("CU", 0, -1, 0), ("CU", 0, -1, 1),
    ("CU", 1, 0, 2), ("Y", 1, 1, 1, 3), ("CU", 0, 1, 0), ("CU", 0, 0, 2), ("Y", -1, 1, 1, 3), ("CU", 0, 0, 3),
    ("YF", -1, 1, 1, 3), ("CU", 1, 1, 0), ("CU", 1, -1, 2), ("CU", 0, 1, 3), ("CU", 0, -1, 2), ("CU", 1, 0, 0),
    ("CU", 1, 1, 2), ("CU", 0, -1, 3), ("CU", 0, 1, 1), ("CU", 0, 2, 2), ("CU", 1, 2, 2), ("CU", 1, -1, 3), ("CU", 1, 1, 3),
    ("CU", 1, 0, 3), ("CU", 0, 2, 3), ("CU", 1, 2, 3),
)


def mod4(v):
    return lax.rem(v + 8, 4)


class Step:
    def __init__(self, refs):
        (self.order, self.occupancy, self.square_pattern, self.cube_pattern, self.p, self.out, self.panel, self.p_cols,
         self.s_cols, self.square, self.cube, self.z_send, self.z_recv, self.e_send, self.x_send, self.x_recv, self.y_send,
         self.y_recv, self.sib_send, self.sib_recv) = refs
        self.y, self.zh, self.zl, self.x, self.core = (lax.axis_index(name) for name in AXES)
        self.z = self.zh * 4 + self.zl
        self.step = self.p.shape[0] // CHUNKS
        self.waited = set()
        self.sent = []
        pair = lax.rem(self.zl, 2)
        half = self.zl // 2
        self.places = (self.zl, self.zl + 1 - 2 * pair, 2 - half, 3 - 3 * half)

    def at_x(self, d):
        return {"x": mod4(self.x + d)}

    def at_y(self, d):
        return {"y": mod4(self.y + d)}

    def at_z(self, d):
        z = lax.rem(self.z + d + 8, 8)
        return {"zh": z // 4, "zl": lax.rem(z, 4)}

    def other_core(self):
        return {"core": 1 - self.core}

    def rows(self, j):
        return pl.ds(j * self.step, self.step)

    def panel_at(self, x, zl, j):
        return self.panel.at[self.core, x * 4 + zl, self.rows(j)]

    def group(self, h, d):
        return 2 * mod4(self.y + d) + (self.zh if h == 0 else 1 - self.zh)

    def cols_at(self, phase, h, d, j):
        return (self.p_cols if phase == 0 else self.s_cols).at[self.group(h, d), self.rows(j)]

    def send(self, src, dst, send_sem, recv_sem, device, guard=None):
        copy = pltpu.make_async_remote_copy(
            src_ref=src, dst_ref=dst, send_sem=send_sem, recv_sem=recv_sem, device_id=device,
            device_id_type=pl.DeviceIdType.MESH)
        if guard is None:
            copy.start()
        else:
            pl.when(guard)(copy.start)
        self.sent.append((copy, guard))

    def arrived(self, key, dst, recv_sem, guard=None):
        if key in self.waited:
            return
        self.waited.add(key)
        copy = pltpu.make_async_remote_copy(
            src_ref=dst, dst_ref=dst, send_sem=recv_sem, recv_sem=recv_sem, device_id=self.other_core(),
            device_id_type=pl.DeviceIdType.MESH)
        if guard is None:
            copy.wait_recv()
        else:
            pl.when(guard)(copy.wait_recv)

    def x_arrived(self, g, j, o):
        self.arrived(("x", g, j, o), self.panel_at(mod4(self.x + g), self.places[o], j), self.x_recv.at[g % 4, j, o])

    def y_arrived(self, phase, h, d, j):
        self.arrived(("y", phase, h, d, j), self.cols_at(phase, h, d, j), self.y_recv.at[phase, h, d % 4, j])

    def Z(self, j, d):
        zl = self.zl
        if d > 0:
            self.arrived(("z", j, d, 0), self.panel_at(self.x, lax.max(zl - d, 0), j), self.z_recv.at[0, j, d], zl >= d)
            self.arrived(("z", j, d, 1), self.panel_at(self.x, lax.min(zl + d, 3), j), self.z_recv.at[1, j, d], zl <= 3 - d)
        if d < 3:
            low = self.panel_at(self.x, lax.max(zl - d, 0), j)
            high = self.panel_at(self.x, lax.min(zl + d, 3), j)
            up, down = (zl >= d) & (zl < 3), (zl <= 3 - d) & (zl > 0)
            self.send(low, low, self.z_send.at[0, j, d], self.z_recv.at[0, j, d + 1], self.at_z(1), up)
            self.send(high, high, self.z_send.at[1, j, d], self.z_recv.at[1, j, d + 1], self.at_z(-1), down)
        if d >= 2:
            far = 4 - d
            mine = self.p_cols.at[2 * self.y + self.zh, self.rows(j)]
            self.send(self.panel_at(self.x, 3 - d, j), mine, self.e_send.at[0, 0, j, far - 1], self.y_recv.at[0, 1, 0, j],
                      self.at_z(far), zl == 3)
            self.send(self.panel_at(self.x, d, j), mine, self.e_send.at[0, 1, j, far - 1], self.y_recv.at[0, 1, 0, j],
                      self.at_z(-far), zl == 0)

    def X(self, sign, j, o):
        tile = self.panel_at(self.x, self.places[o], j)
        self.send(tile, tile, self.x_send.at[(1 - sign) // 2, 0, j, o], self.x_recv.at[-sign % 4, j, o], self.at_x(sign))

    def XF(self, sign, j, o):
        self.x_arrived(-sign, j, o)
        tile = self.panel_at(mod4(self.x - sign), self.places[o], j)
        self.send(tile, tile, self.x_send.at[(1 - sign) // 2, 1, j, o], self.x_recv.at[2, j, o], self.at_x(sign))

    def Y(self, sign, phase, h, j):
        if h == 1:
            self.y_arrived(phase, 1, 0, j)
        tile = self.cols_at(phase, h, 0, j)
        self.send(tile, tile, self.y_send.at[phase, (1 - sign) // 2, h, 0, j], self.y_recv.at[phase, h, -sign % 4, j],
                  self.at_y(sign))

    def YF(self, sign, phase, h, j):
        self.y_arrived(phase, h, -sign, j)
        tile = self.cols_at(phase, h, -sign, j)
        self.send(tile, tile, self.y_send.at[phase, (1 - sign) // 2, h, 1, j], self.y_recv.at[phase, h, 2, j], self.at_y(sign))

    def ES(self, j):
        tile = self.cols_at(1, 0, 0, j)
        self.send(tile, tile, self.e_send.at[1, 0, j, 0], self.y_recv.at[1, 1, 0, j], self.at_z(4))

    def SIB(self, j, g):
        if g != 0:
            for o in range(4):
                self.x_arrived(g, j, o)
        tiles = self.panel.at[self.core, pl.ds(mod4(self.x + g) * 4, 4), self.rows(j)]
        self.send(tiles, tiles, self.sib_send.at[j, g % 4], self.sib_recv.at[j, g % 4], self.other_core())

    def sibling_arrived(self, j):
        for g in (0, -1, 1, 2):
            tiles = self.panel.at[1 - self.core, pl.ds(mod4(self.x + g) * 4, 4), self.rows(j)]
            self.arrived(("s", j, g), tiles, self.sib_recv.at[j, g % 4])

    def SQ(self, j, h):
        for d in (-1, 1, 2):
            for i in range(CHUNKS):
                self.y_arrived(0, h, d, i)
        if h == 1:
            for i in range(CHUNKS):
                self.y_arrived(0, 1, 0, i)
        for g in (-1, 1, 2):
            for o in range(4):
                self.x_arrived(g, j, o)
        self.sibling_arrived(j)
        zh = self.zh if h == 0 else 1 - self.zh

        def add(y, carry):
            total = None
            for t in range(4):
                left = self.panel[t % 2, (2 * zh + t // 2) * 4 + y, self.rows(j), :]
                right = self.p_cols[2 * y + zh, pl.ds(t * 256, 256), :]
                term = jnp.dot(left, right, preferred_element_type=jnp.float32)
                total = term if total is None else total + term
            self.square[self.rows(j), :] += total
            return carry

        lax.fori_loop(0, 4, add, 0)
        if h == 1:
            mine = 2 * self.y + self.zh
            for i, q, keep in self.flags(self.square_pattern, j):
                block = self.square[pl.ds(i * 128, 128), pl.ds(q * 128, 128)] * keep
                self.square[pl.ds(i * 128, 128), pl.ds(q * 128, 128)] = block
                self.s_cols[mine, pl.ds(i * 128, 128), pl.ds(q * 128, 128)] = block.astype(jnp.bfloat16)

    def CU(self, h, d, j):
        if (h, d) != (0, 0):
            self.y_arrived(1, h, d, j)
        zh = self.zh if h == 0 else 1 - self.zh
        y = mod4(self.y + d)
        t = j * self.step // 256
        width = min(self.step, 256)
        inner = pl.ds(j * self.step % 256, width)

        def add(i, carry):
            rows = pl.ds(pl.multiple_of(i * 256, 256), 256)
            left = self.panel[t % 2, (2 * zh + t // 2) * 4 + y, rows, inner]
            right = self.s_cols[2 * y + zh, self.rows(j), :]
            self.cube[rows, :] += jnp.dot(left, right, preferred_element_type=jnp.float32)
            return carry

        lax.fori_loop(0, 4, add, 0)

    def flags(self, pattern, j):
        base_row = (2 * self.y + self.zh) * 8
        base_col = ((self.zl * 4 + self.x) * 2 + self.core) * 2
        count = self.step // 128
        for i in range(j * count, (j + 1) * count):
            a = self.order[base_row + i]
            for q in range(2):
                b = self.order[base_col + q]
                kept = pattern[lax.min(a, b), lax.max(a, b)]
                yield i, q, jnp.where(kept > 0, jnp.float32(1), jnp.float32(0))

    def run(self):
        barrier = pltpu.get_barrier_semaphore()
        partners = [self.at_x(1), self.at_x(-1), self.at_y(1), self.at_y(-1), self.at_z(1), self.at_z(-1), self.at_z(2),
                    self.at_z(-2), self.at_z(4), self.other_core()]
        for device in partners:
            pl.semaphore_signal(barrier, inc=1, device_id=device, device_id_type=pl.DeviceIdType.MESH)
        mine, place = 2 * self.y + self.zh, self.x * 4 + self.zl
        for j in range(CHUNKS):
            for i, q, keep in self.flags(self.occupancy, j):
                block = self.p[pl.ds(i * 128, 128), pl.ds(q * 128, 128)].astype(jnp.float32) * keep
                block = block.astype(jnp.bfloat16)
                self.panel[self.core, place, pl.ds(i * 128, 128), pl.ds(q * 128, 128)] = block
                self.p_cols[mine, pl.ds(i * 128, 128), pl.ds(q * 128, 128)] = block
        self.square[...] = jnp.zeros_like(self.square)
        self.cube[...] = jnp.zeros_like(self.cube)
        pl.semaphore_wait(barrier, len(partners))
        for name, *args in ORDER:
            getattr(self, name)(*args)
        for j in range(CHUNKS):
            for i, q, keep in self.flags(self.cube_pattern, j):
                at = (pl.ds(i * 128, 128), pl.ds(q * 128, 128))
                self.out[at] = 3.0 * self.square[at] - 2.0 * (self.cube[at] * keep)
        for copy, guard in self.sent:
            if guard is None:
                copy.wait_send()
            else:
                pl.when(guard)(copy.wait_send)


def kernel(*refs):
    Step(refs).run()


def body(p_values, occupancy, square_pattern, cube_pattern, block_order):
    rows, cols = p_values.shape
    smem = pl.BlockSpec(memory_space=pltpu.SMEM)
    vmem = pl.BlockSpec(memory_space=pltpu.VMEM)
    sem = pltpu.SemaphoreType.DMA
    return pl.pallas_call(
        kernel,
        out_shape=jax.ShapeDtypeStruct((rows, cols), jnp.float32),
        in_specs=[smem] * 4 + [vmem],
        out_specs=vmem,
        scratch_shapes=[
            pltpu.VMEM((2, 16, rows, cols), jnp.bfloat16),
            pltpu.VMEM((8, rows, cols), jnp.bfloat16),
            pltpu.VMEM((8, rows, cols), jnp.bfloat16),
            pltpu.VMEM((rows, cols), jnp.float32),
            pltpu.VMEM((rows, cols), jnp.float32),
            sem((2, CHUNKS, 3)),
            sem((2, CHUNKS, 4)),
            sem((2, 2, CHUNKS, 2)),
            sem((2, 2, CHUNKS, 4)),
            sem((4, CHUNKS, 4)),
            sem((2, 2, 2, 2, CHUNKS)),
            sem((2, 2, 4, CHUNKS)),
            sem((CHUNKS, 4)),
            sem((CHUNKS, 4)),
        ],
        compiler_params=pltpu.CompilerParams(collective_id=0, has_side_effects=True, vmem_limit_bytes=48 * 2**20),
        cost_estimate=pl.CostEstimate(flops=4 * rows * cols * 8192, bytes_accessed=2**24, transcendentals=0),
    )(block_order, occupancy, square_pattern, cube_pattern, p_values)


def solution(mesh):
    finer = Mesh(mesh.devices.reshape(4, 2, 4, 4, 2), AXES)
    tiles = P(("y", "zh"), ("zl", "x", "core"))
    return jax.shard_map(
        body, mesh=finer, in_specs=(tiles, P(), P(), P(), P()), out_specs=tiles, check_vma=False
    )
```

time: 366 us -> 127 us (0.35)
  waiting for transfers between devices: 314 us -> 0 us
  Pallas kernels: 0 us -> 122 us
  matrix products: 36 us -> 0 us
  between operations: 13.2 us -> 0.01 us
    all_gather x4 -> x0, waiting for transfers between devices: 313 us -> none  [the longest x1 121 us: body(): p_panel = lax.all_gather(p_tile, 'col', axis=1, tiled=True)]
    pallas_call x0 -> x1, Pallas kernels: none -> 122 us  [body(): pl.pallas_call(kernel, out_shape=jax.ShapeDtypeStruct((rows, cols), jnp.f...]
    dot_general x10 -> x0, matrix products: 36 us -> none  [the longest x2 24.7 us: panel_step(): return jnp.dot(p_panel, shard_piece, preferred_element_type=jnp.float32)]
  transfers between devices with their start and end apart: 4 -> 0, of which waited for: 4 -> 0; matrix products, arithmetic and copies ran while one was open for 2% -> 0% of each run, Pallas kernels for 0% -> 0%
where the time goes in v1:
time: 127 us
  Pallas kernels  122 us (96%)
  local copies, waits for them, and re-layouts  4.94 us (4%)
    pallas_call x1, Pallas kernels, body(): pl.pallas_call(kernel, out_shape=jax.ShapeDtypeStruct((rows, cols), jnp.f...  122 us
    unnamed x11, local copies, waits for them, and re-layouts  4.94 us

profile of v1, /device:TPU:1, one launch (start us, length us, event | category | flops | bytes accessed | tf_op | source)
XLA Modules:
  0.0 127.0 jit_solution(9643181945716295753)
XLA Ops:
  0.0 0.0 copy-start
  0.0 1.0 copy-done
  1.0 0.0 copy-start.1
  1.0 0.8 copy-done.1
  1.8 0.0 copy-start.2
  1.8 0.8 copy-done.2
  2.6 0.0 copy-start.3
  2.6 0.8 copy-done.3
  3.3 0.0 copy-start.4
  3.3 0.7 copy-done.4
  4.0 122.0 %shard_map.55 = f32[1024,256]{1,0:T(8,128)S(1)} custom-call(s32[64]{0:T(128)S(1)} %copy-done.4, s32[64,64]{1,0:T(8,128)S(1)} %copy-done.1, s32[64,64]{1,0:T(8,128)S(1)} %copy-done.2, s32[64,64]{1,0:T(8,128)S(1)} %copy-done.3, bf16[1024,256]{1,0:T(8,128)(2,1)S(1)} %copy-done), custom_call_target="tpu_custom_call" | custom-call | flops 8589934592 | bytes 16777216 | tf_op jit(solution)/shard_map/pallas_call | solution.py:267
  126.0 1.0 copy.7
Async XLA Ops:
  0.0 1.0 copy-start
  1.0 0.8 copy-start.1
  1.8 0.8 copy-start.2
  2.6 0.8 copy-start.3
  3.3 0.7 copy-start.4

commit v2 on v1

v2 whole, which is shorter than its diff:
```python
import functools
import jax
import jax.numpy as jnp
from jax import lax
from jax.experimental import pallas as pl
from jax.experimental.pallas import tpu as pltpu
from jax.sharding import Mesh
from jax.sharding import PartitionSpec as P

AXES = ("y", "zh", "zl", "x", "core")
CHUNKS = 8
X_FIRST = (7,)
SPAN = 2
SOURCES = (((0, 0), (0, -1), (0, 1)), ((1, 0), (0, 2)), ((1, -1), (1, 1)), ((1, 2),))
ORDER = (
    ("ZP", 4), ("X", -1, 0, 0), ("X", 1, 4, 0), ("Y", -1, 0, 0, 1), ("Y", -1, 0, 0, 3), ("X", -1, 2, 0), ("X", -1, 4, 0),
    ("Z", 1, 0), ("ZP", 1), ("X", 1, 5, 0), ("X", -1, 7, 0), ("Z", 4, 0), ("X", 1, 7, 0), ("X", 1, 1, 0), ("Z", 2, 0),
    ("X", -1, 3, 0), ("Z", 3, 0), ("ZP", 2), ("XF", 1, 4, 0), ("ZP", 3), ("Y", -1, 0, 0, 7), ("X", 1, 2, 0),
    ("Y", 1, 0, 0, 2), ("Y", 1, 0, 0, 6), ("Y", 1, 0, 0, 4), ("X", -1, 1, 0), ("Y", -1, 0, 0, 0), ("Z", 4, 1),
    ("YF", -1, 0, 0, 3), ("YF", -1, 0, 0, 7), ("Z", 2, 1), ("Y", 1, 0, 0, 7), ("Y", -1, 0, 0, 2), ("Y", -1, 0, 0, 5),
    ("YF", -1, 0, 0, 1), ("Z", 3, 1), ("X", -1, 2, 1), ("X", 1, 3, 0), ("X", -1, 4, 1), ("YF", 1, 0, 0, 2), ("Z", 4, 2),
    ("Z", 7, 0), ("X", 1, 3, 1), ("Z", 0, 0), ("Z", 2, 2), ("X", -1, 5, 0), ("Y", 1, 0, 0, 5), ("X", 1, 2, 1),
    ("X", -1, 2, 2), ("Y", -1, 0, 0, 4), ("ZP", 0), ("Y", 1, 0, 0, 0), ("Z", 1, 1), ("XF", 1, 3, 0), ("X", -1, 4, 2),
    ("Z", 3, 2), ("X", 1, 0, 0), ("Z", 4, 3), ("XF", 1, 2, 0), ("X", -1, 1, 1), ("Z", 2, 3), ("XH", -1, 7), ("X", -1, 2, 3),
    ("Z", 5, 0), ("X", 1, 2, 2), ("SIB", 4, 0), ("X", -1, 4, 3), ("ZP", 5), ("X", 1, 4, 1), ("XH", 1, 7), ("YF", 1, 0, 0, 0),
    ("Z", 3, 3), ("Z", 6, 0), ("Z", 1, 2), ("SIB", 2, 0), ("Z", 0, 1), ("YF", 1, 0, 0, 6), ("YF", 1, 0, 0, 4), ("X", 1, 3, 2),
    ("Y", -1, 0, 1, 2), ("Y", 1, 0, 1, 4), ("Y", -1, 0, 0, 6), ("Z", 5, 1), ("X", -1, 0, 1), ("X", -1, 3, 3), ("X", 1, 4, 3),
    ("Z", 1, 3), ("Z", 0, 2), ("X", 1, 2, 3), ("X", -1, 1, 2), ("X", 1, 3, 3), ("Z", 5, 2), ("SIB", 3, 0), ("X", 1, 4, 2),
    ("ZP", 6), ("Y", 1, 0, 1, 3), ("X", -1, 3, 2), ("X", 1, 0, 1), ("Y", -1, 0, 1, 1), ("X", -1, 0, 2), ("Y", 1, 0, 1, 2),
    ("Y", 1, 0, 0, 3), ("SIB", 1, 0), ("Z", 0, 3), ("X", -1, 0, 3), ("XF", -1, 2, 2), ("X", 1, 1, 1), ("Z", 5, 3),
    ("Y", -1, 0, 1, 3), ("Y", 1, 0, 0, 1), ("YF", 1, 0, 1, 4), ("SIB", 2, 1), ("ZP", 7), ("YF", -1, 0, 0, 5), ("X", 1, 0, 2),
    ("X", -1, 3, 1), ("XF", -1, 2, 3), ("XF", 1, 3, 1), ("XF", 1, 2, 1), ("SIB", 2, -1), ("X", -1, 1, 3), ("X", 1, 1, 2),
    ("Y", 1, 0, 1, 1), ("Z", 6, 1), ("Y", -1, 0, 1, 0), ("XF", -1, 3, 3), ("X", 1, 0, 3), ("YF", -1, 0, 1, 1), ("Z", 7, 1),
    ("XF", -1, 3, 2), ("YF", -1, 0, 1, 3), ("SIB", 0, 1), ("Z", 6, 2), ("YF", 1, 0, 1, 2), ("XF", 1, 0, 1), ("Z", 7, 2),
    ("XF", 1, 0, 0), ("SIB", 3, -1), ("XF", -1, 0, 2), ("Z", 6, 3), ("Y", -1, 0, 1, 5), ("XF", -1, 0, 3), ("Y", 1, 0, 1, 5),
    ("XF", 1, 4, 1), ("ZT", 2, 7, 0), ("XF", -1, 4, 3), ("XF", 1, 1, 1), ("SIB", 3, 1), ("ZT", -1, 7, 0), ("X", 1, 1, 3),
    ("Y", 1, 0, 1, 0), ("Z", 7, 3), ("XF", -1, 4, 2), ("ZT", 1, 7, 0), ("Y", -1, 0, 1, 4), ("X", 1, 5, 2), ("XF", 1, 1, 0),
    ("Y", -1, 0, 1, 6), ("SIB", 0, 0), ("SIB", 2, 2), ("Y", 1, 0, 1, 6), ("Y", -1, 0, 1, 7), ("ZT", 2, 7, 1), ("X", 1, 5, 1),
    ("X", 1, 6, 0), ("Y", 1, 0, 1, 7), ("ZT", -1, 7, 1), ("YF", -1, 0, 1, 5), ("SIB", 3, 2), ("SIB", 4, -1),
    ("YF", 1, 0, 1, 0), ("YF", 1, 0, 1, 6), ("SQ", 2, 0), ("ZT", 1, 7, 1), ("X", -1, 5, 3), ("X", 1, 5, 3), ("ZT", 2, 7, 2),
    ("XF", -1, 1, 3), ("YF", -1, 0, 1, 7), ("SIB", 7, 0), ("SQ", 3, 0), ("SIB", 1, 1), ("SIB", 0, -1), ("XF", -1, 1, 2),
    ("ZT", -1, 7, 2), ("X", -1, 6, 3), ("SIB", 0, 2), ("X", -1, 5, 2), ("X", -1, 6, 2), ("X", -1, 5, 1), ("SIB", 4, 1),
    ("SQ", 3, 1), ("X", 1, 6, 1), ("SQ", 2, 1), ("SIB", 4, 2), ("ZT", 1, 7, 2), ("SQ", 3, 2), ("ZT", 2, 7, 3),
    ("Y", -1, 1, 0, 3), ("Y", 1, 1, 0, 3), ("SQ", 2, 2), ("ES", 2), ("Y", 1, 1, 0, 2), ("SIB", 7, 2), ("Y", -1, 1, 0, 2),
    ("SQ", 0, 0), ("SQ", 0, 1), ("ZT", -1, 7, 3), ("SQ", 0, 2), ("Y", -1, 1, 0, 0), ("SIB", 7, -1), ("Y", 1, 1, 0, 0),
    ("ES", 3), ("ZT", 1, 7, 3), ("SIB", 7, 1), ("SQ", 4, 0), ("SQ", 4, 1), ("SQ", 4, 2), ("YF", -1, 1, 0, 3),
    ("Y", 1, 1, 0, 4), ("ES", 4), ("SIB", 1, -1), ("ES", 0), ("XF", 1, 5, 0), ("Y", -1, 1, 0, 4), ("YF", 1, 1, 0, 2),
    ("SIB", 1, 2), ("SQ", 7, 0), ("SQ", 7, 1), ("SQ", 7, 2), ("Y", -1, 1, 0, 7), ("XF", -1, 5, 3), ("Y", -1, 1, 1, 2),
    ("XF", -1, 5, 2), ("Y", 1, 1, 1, 2), ("SQ", 1, 0), ("XF", 1, 5, 1), ("YF", 1, 1, 0, 4), ("SQ", 1, 1), ("X", 1, 6, 2),
    ("SQ", 1, 2), ("X", -1, 6, 0), ("Y", 1, 1, 0, 7), ("ES", 1), ("SIB", 5, -1), ("Y", -1, 1, 0, 1), ("Y", -1, 1, 1, 3),
    ("YF", -1, 1, 0, 7), ("SIB", 5, 1), ("YF", 1, 1, 1, 2), ("SIB", 6, 0), ("X", 1, 6, 3), ("SIB", 5, 0), ("X", -1, 6, 1),
    ("XF", -1, 6, 2), ("XF", -1, 6, 3), ("SIB", 5, 2), ("Y", 1, 1, 1, 3), ("XF", 1, 6, 1), ("ES", 7), ("Y", -1, 1, 1, 4),
    ("Y", 1, 1, 0, 1), ("XF", 1, 6, 0), ("YF", -1, 1, 0, 1), ("SQ", 5, 0), ("Y", 1, 1, 1, 0), ("SQ", 5, 1), ("SIB", 6, -1),
    ("SQ", 5, 2), ("YF", 1, 1, 0, 0), ("SIB", 6, 1), ("Y", 1, 1, 0, 5), ("YF", -1, 1, 1, 3), ("ES", 5), ("SIB", 6, 2),
    ("Y", 1, 1, 1, 1), ("Y", -1, 1, 1, 0), ("Y", -1, 1, 0, 5), ("Y", -1, 1, 1, 1), ("Y", 1, 1, 1, 4), ("SQ", 6, 0),
    ("SQ", 6, 1), ("SQ", 6, 2), ("Y", -1, 1, 1, 7), ("ES", 6), ("CU", 2, 1), ("Y", 1, 1, 0, 6), ("CU", 1, 0),
    ("Y", 1, 1, 1, 7), ("CU", 1, 1), ("YF", -1, 1, 0, 5), ("CU", 3, 1), ("Y", -1, 1, 0, 6), ("Y", 1, 1, 1, 5),
    ("Y", -1, 1, 1, 5), ("CU", 0, 1), ("YF", 1, 1, 0, 6), ("YF", -1, 1, 1, 1), ("CU", 0, 0), ("CU", 0, 2), ("Y", 1, 1, 1, 6),
    ("CU", 1, 2), ("YF", 1, 1, 1, 0), ("Y", -1, 1, 1, 6), ("CU", 0, 3), ("CU", 2, 0), ("YF", -1, 1, 1, 5), ("YF", 1, 1, 1, 4),
    ("CU", 1, 3), ("CU", 2, 2), ("YF", -1, 1, 1, 7), ("YF", 1, 1, 1, 6), ("CU", 2, 3), ("CU", 3, 0), ("CU", 3, 2),
    ("CU", 3, 3),
)


def mod4(v):
    return lax.rem(v + 8, 4)


class Step:
    def __init__(self, refs):
        (self.order_in, self.occupancy_in, self.square_in, self.cube_in, self.p_in, self.out, self.order, self.occupancy,
         self.square_pattern, self.cube_pattern, self.panel, self.p_cols, self.s_cols, self.square, self.cube, self.in_sem,
         self.send_sem, self.z_recv, self.x_recv, self.y_recv, self.sib_recv) = refs
        self.y, self.zh, self.zl, self.x, self.core = (lax.axis_index(name) for name in AXES)
        self.step = self.panel.shape[2] // CHUNKS
        self.waited = set()
        pair = lax.rem(self.zl, 2)
        half = self.zl // 2
        self.places = (self.zl, self.zl + 1 - 2 * pair, 2 - half, 3 - 3 * half)

    def at_x(self, d):
        return {"x": mod4(self.x + d)}

    def at_y(self, d):
        return {"y": mod4(self.y + d)}

    def at_z(self, d):
        z = lax.rem(self.zh * 4 + self.zl + d + 8, 8)
        return {"zh": z // 4, "zl": lax.rem(z, 4)}

    def other_core(self):
        return {"core": 1 - self.core}

    def rows(self, j):
        return pl.ds(j * self.step, self.step)

    def half_rows(self, j, sign):
        return pl.ds(j * self.step + (0 if sign > 0 else self.step // 2), self.step // 2)

    def panel_at(self, g, zl, j):
        return self.panel.at[self.core, mod4(self.x + g) * 4 + zl, self.rows(j)]

    def half_at(self, g, j, sign):
        return self.panel.at[self.core, mod4(self.x + g) * 4 + self.zl, self.half_rows(j, sign)]

    def group(self, h, d):
        return 2 * mod4(self.y + d) + (self.zh if h == 0 else 1 - self.zh)

    def cols_at(self, phase, h, d, j):
        return (self.p_cols if phase == 0 else self.s_cols).at[self.group(h, d), self.rows(j)]

    def send(self, src, dst, kind, recv_sem, device, guard=None):
        copy = pltpu.make_async_remote_copy(
            src_ref=src, dst_ref=dst, send_sem=self.send_sem.at[kind], recv_sem=recv_sem, device_id=device,
            device_id_type=pl.DeviceIdType.MESH)
        if guard is None:
            copy.start()
        else:
            pl.when(guard)(copy.start)

    def arrived(self, key, dst, recv_sem, guard=None):
        if key in self.waited:
            return
        self.waited.add(key)
        copy = pltpu.make_async_remote_copy(
            src_ref=dst, dst_ref=dst, send_sem=recv_sem, recv_sem=recv_sem, device_id=self.other_core(),
            device_id_type=pl.DeviceIdType.MESH)
        if guard is None:
            copy.wait_recv()
        else:
            pl.when(guard)(copy.wait_recv)

    def sends_done(self, kind, tiles, rows, guard=None):
        part = self.panel.at[0, pl.ds(0, tiles), pl.ds(0, rows)]
        copy = pltpu.make_async_remote_copy(
            src_ref=part, dst_ref=part, send_sem=self.send_sem.at[kind], recv_sem=self.send_sem.at[kind],
            device_id=self.other_core(), device_id_type=pl.DeviceIdType.MESH)
        if guard is None:
            copy.wait_send()
        else:
            pl.when(guard)(copy.wait_send)

    def all_sends_done(self):
        step, first = self.step, len(X_FIRST)
        plain = CHUNKS - first
        end = (self.zl == 0) | (self.zl == 3)
        middle = (self.zl == 1) | (self.zl == 2)
        self.sends_done(0, plain, 8 * step)
        self.sends_done(1, plain, 4 * step)
        self.sends_done(2, 3, CHUNKS * step, end)
        self.sends_done(2, 5, CHUNKS * step, middle)
        self.sends_done(3, 6, CHUNKS * step)
        self.sends_done(4, 6, CHUNKS * step)
        self.sends_done(5, 1, CHUNKS * step)
        self.sends_done(6, 16, CHUNKS * step)
        if first:
            self.sends_done(7, 3 * first, step)
            self.sends_done(8, 3 * first, step, end)
            self.sends_done(8, 15 * first, step, middle)

    def x_arrived(self, g, j, o):
        self.arrived(("x", g, j, o), self.panel_at(g, self.places[o], j), self.x_recv.at[g % 4 - 1, j, o])

    def half_arrived(self, j, sign):
        self.arrived(("h", j, sign), self.half_at(2, j, sign), self.x_recv.at[1, j, (1 - sign) // 2])

    def group_arrived(self, g, j):
        if j not in X_FIRST:
            for o in range(4):
                self.x_arrived(g, j, o)
        elif g == 2:
            self.half_arrived(j, 1)
            self.half_arrived(j, -1)
        else:
            self.x_arrived(g, j, 0)

    def y_arrived(self, phase, h, d, j):
        self.arrived(("y", phase, h, d, j), self.cols_at(phase, h, d, j), self.y_recv.at[phase, h, d % 4, j])

    def line(self, g, j, d, kind, at):
        zl = self.zl
        low = self.panel_at(g, lax.max(zl - d, 0), j)
        high = self.panel_at(g, lax.min(zl + d, 3), j)
        if d > 0:
            self.arrived(("z", g, j, d, 0), low, self.z_recv.at[0, at, d - 1], zl >= d)
            self.arrived(("z", g, j, d, 1), high, self.z_recv.at[1, at, d - 1], zl <= 3 - d)
        if d < 3:
            self.send(low, low, kind, self.z_recv.at[0, at, d], self.at_z(1), (zl >= d) & (zl < 3))
            self.send(high, high, kind, self.z_recv.at[1, at, d], self.at_z(-1), (zl <= 3 - d) & (zl > 0))

    def Z(self, j, d):
        if d == 0:
            tile = self.panel_at(0, self.zl, j)
            self.send(tile, tile, 2, self.z_recv.at[0, j, 0], self.at_z(1), self.zl < 2)
            self.send(tile, tile, 2, self.z_recv.at[1, j, 0], self.at_z(-1), self.zl >= 2)
            return
        self.line(0, j, d, 2, j)
        if d >= 2:
            far = 4 - d
            mine = self.p_cols.at[self.group(0, 0), self.rows(j)]
            self.send(self.panel_at(0, 3 - d, j), mine, 2, self.y_recv.at[0, 1, 0, j], self.at_z(far), self.zl == 3)
            self.send(self.panel_at(0, d, j), mine, 2, self.y_recv.at[0, 1, 0, j], self.at_z(-far), self.zl == 0)

    def ZP(self, j):
        tile = self.panel_at(0, self.zl, j)
        self.send(tile, tile, 2, self.z_recv.at[1, j, 0], self.at_z(-1), self.zl == 1)
        self.send(tile, tile, 2, self.z_recv.at[0, j, 0], self.at_z(1), self.zl == 2)

    def ZT(self, g, j, d):
        if d == 0:
            self.group_arrived(g, j)
        self.line(g, j, d, 8, CHUNKS + 3 * X_FIRST.index(j) + g % 4 - 1)

    def X(self, sign, j, o):
        tile = self.panel_at(0, self.places[o], j)
        self.send(tile, tile, 7 if j in X_FIRST else 0, self.x_recv.at[-sign % 4 - 1, j, o], self.at_x(sign))

    def XF(self, sign, j, o):
        self.x_arrived(-sign, j, o)
        tile = self.panel_at(-sign, self.places[o], j)
        self.send(tile, tile, 1, self.x_recv.at[1, j, o], self.at_x(sign))

    def XH(self, sign, j):
        self.x_arrived(-sign, j, 0)
        tile = self.half_at(-sign, j, sign)
        self.send(tile, tile, 7, self.x_recv.at[1, j, (1 - sign) // 2], self.at_x(sign))

    def Y(self, sign, phase, h, j):
        if h == 1:
            self.y_arrived(phase, 1, 0, j)
        tile = self.cols_at(phase, h, 0, j)
        self.send(tile, tile, 3 + phase, self.y_recv.at[phase, h, -sign % 4, j], self.at_y(sign))

    def YF(self, sign, phase, h, j):
        self.y_arrived(phase, h, -sign, j)
        tile = self.cols_at(phase, h, -sign, j)
        self.send(tile, tile, 3 + phase, self.y_recv.at[phase, h, 2, j], self.at_y(sign))

    def ES(self, j):
        tile = self.cols_at(1, 0, 0, j)
        self.send(tile, tile, 5, self.y_recv.at[1, 1, 0, j], self.at_z(4))

    def SIB(self, j, g):
        if g != 0:
            self.group_arrived(g, j)
        tiles = self.panel.at[self.core, pl.ds(mod4(self.x + g) * 4, 4), self.rows(j)]
        self.send(tiles, tiles, 6, self.sib_recv.at[j, g % 4], self.other_core())

    def sibling_arrived(self, j):
        for g in (0, -1, 1, 2):
            tiles = self.panel.at[1 - self.core, pl.ds(mod4(self.x + g) * 4, 4), self.rows(j)]
            self.arrived(("s", j, g), tiles, self.sib_recv.at[j, g % 4])

    def square_terms(self, j, y, zh):
        total = None
        for t in range(4):
            left = self.panel[t % 2, (2 * zh + t // 2) * 4 + y, self.rows(j), :]
            right = self.p_cols[2 * y + zh, pl.ds(t * 256, 256), :]
            term = jnp.dot(left, right, preferred_element_type=jnp.float32)
            total = term if total is None else total + term
        return total

    def SQ(self, j, part):
        h = min(part, 1)
        for d in ((-1, 1, 2), (0, -1, 1), (2,))[part]:
            for i in range(CHUNKS):
                self.y_arrived(0, h, d, i)
        if part == 0:
            self.sibling_arrived(j)
        zh = self.zh if h == 0 else 1 - self.zh
        first, count = ((0, 4), (self.y - 1, 3), (self.y + 2, 1))[part]

        def add(i, carry):
            self.square[self.rows(j), :] += self.square_terms(j, mod4(first + i), zh)
            return carry

        lax.fori_loop(0, count, add, 0)
        if part == 2:
            mine = self.group(0, 0)
            for i, q, keep in self.flags(self.square_pattern, j):
                at = (pl.ds(i * 128, 128), pl.ds(q * 128, 128))
                block = self.square[at] * keep
                self.square[at] = block
                self.s_cols[(mine,) + at] = block.astype(jnp.bfloat16)

    def CU(self, sources, j):
        terms = []
        for h, d in SOURCES[sources]:
            for i in range(j * SPAN, (j + 1) * SPAN):
                if (h, d) != (0, 0):
                    self.y_arrived(1, h, d, i)
            terms.append((mod4(self.y + d), self.zh if h == 0 else 1 - self.zh))

        def add(i, carry):
            rows = pl.ds(pl.multiple_of(i * 256, 256), 256)
            total = None
            for y, zh in terms:
                left = self.panel[j % 2, (2 * zh + j // 2) * 4 + y, rows, :]
                right = self.s_cols[2 * y + zh, pl.ds(j * 256, 256), :]
                term = jnp.dot(left, right, preferred_element_type=jnp.float32)
                total = term if total is None else total + term
            self.cube[rows, :] += total
            return carry

        lax.fori_loop(0, 4, add, 0)

    def flags(self, pattern, j):
        base_row = self.group(0, 0) * 8
        base_col = ((self.zl * 4 + self.x) * 2 + self.core) * 2
        count = self.step // 128
        for i in range(j * count, (j + 1) * count):
            a = self.order[base_row + i]
            for q in range(2):
                b = self.order[base_col + q]
                kept = pattern[lax.min(a, b), lax.max(a, b)]
                yield i, q, jnp.where(kept > 0, jnp.float32(1), jnp.float32(0))

    def run(self):
        mine, place = self.group(0, 0), self.x * 4 + self.zl
        inputs = [
            pltpu.make_async_copy(src, dst, self.in_sem.at[i]) for i, (src, dst) in enumerate((
                (self.order_in, self.order), (self.occupancy_in, self.occupancy),
                (self.p_in, self.panel.at[self.core, place]),
                (self.square_in, self.square_pattern), (self.cube_in, self.cube_pattern)))]
        for copy in inputs:
            copy.start()
        barrier = pltpu.get_barrier_semaphore()
        partners = [self.at_x(1), self.at_x(-1), self.at_y(1), self.at_y(-1), self.at_z(1), self.at_z(-1), self.at_z(2),
                    self.at_z(-2), self.at_z(4), self.other_core()]
        for device in partners:
            pl.semaphore_signal(barrier, inc=1, device_id=device, device_id_type=pl.DeviceIdType.MESH)
        for copy in inputs:
            copy.wait()
        for j in range(CHUNKS):
            for i, q, keep in self.flags(self.occupancy, j):
                at = (pl.ds(i * 128, 128), pl.ds(q * 128, 128))
                block = (self.panel[(self.core, place) + at].astype(jnp.float32) * keep).astype(jnp.bfloat16)
                self.panel[(self.core, place) + at] = block
                self.p_cols[(mine,) + at] = block
        self.square[...] = jnp.zeros_like(self.square)
        self.cube[...] = jnp.zeros_like(self.cube)
        pl.semaphore_wait(barrier, len(partners))
        for name, *args in ORDER:
            getattr(self, name)(*args)
        for j in range(CHUNKS):
            for i, q, keep in self.flags(self.cube_pattern, j):
                at = (pl.ds(i * 128, 128), pl.ds(q * 128, 128))
                self.out[at] = 3.0 * self.square[at] - 2.0 * (self.cube[at] * keep)
        self.all_sends_done()


def kernel(*refs):
    Step(refs).run()


def body(p_values, occupancy, square_pattern, cube_pattern, block_order):
    rows, cols = p_values.shape
    hbm = pl.BlockSpec(memory_space=pltpu.HBM)
    sem = pltpu.SemaphoreType.DMA
    lines = CHUNKS + 3 * len(X_FIRST)
    return pl.pallas_call(
        kernel,
        out_shape=jax.ShapeDtypeStruct((rows, cols), jnp.float32),
        in_specs=[hbm] * 5,
        out_specs=pl.BlockSpec(memory_space=pltpu.VMEM),
        scratch_shapes=[
            pltpu.SMEM(block_order.shape, jnp.int32),
            pltpu.SMEM(occupancy.shape, jnp.int32),
            pltpu.SMEM(occupancy.shape, jnp.int32),
            pltpu.SMEM(occupancy.shape, jnp.int32),
            pltpu.VMEM((2, 16, rows, cols), jnp.bfloat16),
            pltpu.VMEM((8, rows, cols), jnp.bfloat16),
            pltpu.VMEM((8, rows, cols), jnp.bfloat16),
            pltpu.VMEM((rows, cols), jnp.float32),
            pltpu.VMEM((rows, cols), jnp.float32),
            sem((5,)),
            sem((9,)),
            sem((2, lines, 3)),
            sem((3, CHUNKS, 4)),
            sem((2, 2, 4, CHUNKS)),
            sem((CHUNKS, 4)),
        ],
        compiler_params=pltpu.CompilerParams(collective_id=0, has_side_effects=True, vmem_limit_bytes=48 * 2**20),
        cost_estimate=pl.CostEstimate(flops=4 * rows * cols * 8192, bytes_accessed=2**24, transcendentals=0),
    )(block_order, occupancy, square_pattern, cube_pattern, p_values)


def solution(mesh):
    finer = Mesh(mesh.devices.reshape(4, 2, 4, 4, 2), AXES)
    tiles = P(("y", "zh"), ("zl", "x", "core"))
    return jax.shard_map(
        body, mesh=finer, in_specs=(tiles, P(), P(), P(), P()), out_specs=tiles, check_vma=False
    )
```

time: 127 us -> 109 us (0.86)
  Pallas kernels: 122 us -> 104 us
    pallas_call x1, Pallas kernels: 122 us -> 104 us  [body(): pl.pallas_call(kernel, out_shape=jax.ShapeDtypeStruct((rows, cols), jnp.f...]
where the time goes in v2:
time: 109 us
  Pallas kernels  104 us (95%)
  local copies, waits for them, and re-layouts  4.94 us (5%)
    pallas_call x1, Pallas kernels, body(): pl.pallas_call(kernel, out_shape=jax.ShapeDtypeStruct((rows, cols), jnp.f...  104 us
    unnamed x11, local copies, waits for them, and re-layouts  4.94 us

profile of v2, /device:TPU:1, one launch (start us, length us, event | category | flops | bytes accessed | tf_op | source)
XLA Modules:
  0.0 109.1 jit_solution(998107930716726997)
XLA Ops:
  0.0 0.0 copy-start
  0.0 1.0 copy-done
  1.0 0.0 copy-start.1
  1.0 0.8 copy-done.1
  1.8 0.0 copy-start.2
  1.8 0.8 copy-done.2
  2.6 0.0 copy-start.3
  2.6 0.8 copy-done.3
  3.3 0.0 copy-start.4
  3.3 0.7 copy-done.4
  4.0 104.1 %shard_map.55 = f32[1024,256]{1,0:T(8,128)S(1)} custom-call(s32[64]{0:T(128)S(1)} %copy-done.4, s32[64,64]{1,0:T(8,128)S(1)} %copy-done.1, s32[64,64]{1,0:T(8,128)S(1)} %copy-done.2, s32[64,64]{1,0:T(8,128)S(1)} %copy-done.3, bf16[1024,256]{1,0:T(8,128)(2,1)S(1)} %copy-done), custom_call_target="tpu_custom_call" | custom-call | flops 8589934592 | bytes 16777216 | tf_op jit(solution)/shard_map/pallas_call | solution.py:361
  108.1 1.0 copy.7
Async XLA Ops:
  0.0 1.0 copy-start
  1.0 0.8 copy-start.1
  1.8 0.8 copy-start.2
  2.6 0.8 copy-start.3
  3.3 0.7 copy-start.4

commit v3 on v2

--- a/solution.py
+++ b/solution.py
@@ -13,52 +13,52 @@
 SPAN = 2
 SOURCES = (((0, 0), (0, -1), (0, 1)), ((1, 0), (0, 2)), ((1, -1), (1, 1)), ((1, 2),))
 ORDER = (
-    ("ZP", 4), ("X", -1, 0, 0), ("X", 1, 4, 0), ("Y", -1, 0, 0, 1), ("Y", -1, 0, 0, 3), ("X", -1, 2, 0), ("X", -1, 4, 0),
-    ("Z", 1, 0), ("ZP", 1), ("X", 1, 5, 0), ("X", -1, 7, 0), ("Z", 4, 0), ("X", 1, 7, 0), ("X", 1, 1, 0), ("Z", 2, 0),
-    ("X", -1, 3, 0), ("Z", 3, 0), ("ZP", 2), ("XF", 1, 4, 0), ("ZP", 3), ("Y", -1, 0, 0, 7), ("X", 1, 2, 0),
-    ("Y", 1, 0, 0, 2), ("Y", 1, 0, 0, 6), ("Y", 1, 0, 0, 4), ("X", -1, 1, 0), ("Y", -1, 0, 0, 0), ("Z", 4, 1),
-    ("YF", -1, 0, 0, 3), ("YF", -1, 0, 0, 7), ("Z", 2, 1), ("Y", 1, 0, 0, 7), ("Y", -1, 0, 0, 2), ("Y", -1, 0, 0, 5),
-    ("YF", -1, 0, 0, 1), ("Z", 3, 1), ("X", -1, 2, 1), ("X", 1, 3, 0), ("X", -1, 4, 1), ("YF", 1, 0, 0, 2), ("Z", 4, 2),
-    ("Z", 7, 0), ("X", 1, 3, 1), ("Z", 0, 0), ("Z", 2, 2), ("X", -1, 5, 0), ("Y", 1, 0, 0, 5), ("X", 1, 2, 1),
-    ("X", -1, 2, 2), ("Y", -1, 0, 0, 4), ("ZP", 0), ("Y", 1, 0, 0, 0), ("Z", 1, 1), ("XF", 1, 3, 0), ("X", -1, 4, 2),
-    ("Z", 3, 2), ("X", 1, 0, 0), ("Z", 4, 3), ("XF", 1, 2, 0), ("X", -1, 1, 1), ("Z", 2, 3), ("XH", -1, 7), ("X", -1, 2, 3),
-    ("Z", 5, 0), ("X", 1, 2, 2), ("SIB", 4, 0), ("X", -1, 4, 3), ("ZP", 5), ("X", 1, 4, 1), ("XH", 1, 7), ("YF", 1, 0, 0, 0),
-    ("Z", 3, 3), ("Z", 6, 0), ("Z", 1, 2), ("SIB", 2, 0), ("Z", 0, 1), ("YF", 1, 0, 0, 6), ("YF", 1, 0, 0, 4), ("X", 1, 3, 2),
-    ("Y", -1, 0, 1, 2), ("Y", 1, 0, 1, 4), ("Y", -1, 0, 0, 6), ("Z", 5, 1), ("X", -1, 0, 1), ("X", -1, 3, 3), ("X", 1, 4, 3),
-    ("Z", 1, 3), ("Z", 0, 2), ("X", 1, 2, 3), ("X", -1, 1, 2), ("X", 1, 3, 3), ("Z", 5, 2), ("SIB", 3, 0), ("X", 1, 4, 2),
-    ("ZP", 6), ("Y", 1, 0, 1, 3), ("X", -1, 3, 2), ("X", 1, 0, 1), ("Y", -1, 0, 1, 1), ("X", -1, 0, 2), ("Y", 1, 0, 1, 2),
-    ("Y", 1, 0, 0, 3), ("SIB", 1, 0), ("Z", 0, 3), ("X", -1, 0, 3), ("XF", -1, 2, 2), ("X", 1, 1, 1), ("Z", 5, 3),
-    ("Y", -1, 0, 1, 3), ("Y", 1, 0, 0, 1), ("YF", 1, 0, 1, 4), ("SIB", 2, 1), ("ZP", 7), ("YF", -1, 0, 0, 5), ("X", 1, 0, 2),
-    ("X", -1, 3, 1), ("XF", -1, 2, 3), ("XF", 1, 3, 1), ("XF", 1, 2, 1), ("SIB", 2, -1), ("X", -1, 1, 3), ("X", 1, 1, 2),
-    ("Y", 1, 0, 1, 1), ("Z", 6, 1), ("Y", -1, 0, 1, 0), ("XF", -1, 3, 3), ("X", 1, 0, 3), ("YF", -1, 0, 1, 1), ("Z", 7, 1),
-    ("XF", -1, 3, 2), ("YF", -1, 0, 1, 3), ("SIB", 0, 1), ("Z", 6, 2), ("YF", 1, 0, 1, 2), ("XF", 1, 0, 1), ("Z", 7, 2),
-    ("XF", 1, 0, 0), ("SIB", 3, -1), ("XF", -1, 0, 2), ("Z", 6, 3), ("Y", -1, 0, 1, 5), ("XF", -1, 0, 3), ("Y", 1, 0, 1, 5),
-    ("XF", 1, 4, 1), ("ZT", 2, 7, 0), ("XF", -1, 4, 3), ("XF", 1, 1, 1), ("SIB", 3, 1), ("ZT", -1, 7, 0), ("X", 1, 1, 3),
-    ("Y", 1, 0, 1, 0), ("Z", 7, 3), ("XF", -1, 4, 2), ("ZT", 1, 7, 0), ("Y", -1, 0, 1, 4), ("X", 1, 5, 2), ("XF", 1, 1, 0),
-    ("Y", -1, 0, 1, 6), ("SIB", 0, 0), ("SIB", 2, 2), ("Y", 1, 0, 1, 6), ("Y", -1, 0, 1, 7), ("ZT", 2, 7, 1), ("X", 1, 5, 1),
-    ("X", 1, 6, 0), ("Y", 1, 0, 1, 7), ("ZT", -1, 7, 1), ("YF", -1, 0, 1, 5), ("SIB", 3, 2), ("SIB", 4, -1),
-    ("YF", 1, 0, 1, 0), ("YF", 1, 0, 1, 6), ("SQ", 2, 0), ("ZT", 1, 7, 1), ("X", -1, 5, 3), ("X", 1, 5, 3), ("ZT", 2, 7, 2),
-    ("XF", -1, 1, 3), ("YF", -1, 0, 1, 7), ("SIB", 7, 0), ("SQ", 3, 0), ("SIB", 1, 1), ("SIB", 0, -1), ("XF", -1, 1, 2),
-    ("ZT", -1, 7, 2), ("X", -1, 6, 3), ("SIB", 0, 2), ("X", -1, 5, 2), ("X", -1, 6, 2), ("X", -1, 5, 1), ("SIB", 4, 1),
-    ("SQ", 3, 1), ("X", 1, 6, 1), ("SQ", 2, 1), ("SIB", 4, 2), ("ZT", 1, 7, 2), ("SQ", 3, 2), ("ZT", 2, 7, 3),
-    ("Y", -1, 1, 0, 3), ("Y", 1, 1, 0, 3), ("SQ", 2, 2), ("ES", 2), ("Y", 1, 1, 0, 2), ("SIB", 7, 2), ("Y", -1, 1, 0, 2),
-    ("SQ", 0, 0), ("SQ", 0, 1), ("ZT", -1, 7, 3), ("SQ", 0, 2), ("Y", -1, 1, 0, 0), ("SIB", 7, -1), ("Y", 1, 1, 0, 0),
-    ("ES", 3), ("ZT", 1, 7, 3), ("SIB", 7, 1), ("SQ", 4, 0), ("SQ", 4, 1), ("SQ", 4, 2), ("YF", -1, 1, 0, 3),
-    ("Y", 1, 1, 0, 4), ("ES", 4), ("SIB", 1, -1), ("ES", 0), ("XF", 1, 5, 0), ("Y", -1, 1, 0, 4), ("YF", 1, 1, 0, 2),
-    ("SIB", 1, 2), ("SQ", 7, 0), ("SQ", 7, 1), ("SQ", 7, 2), ("Y", -1, 1, 0, 7), ("XF", -1, 5, 3), ("Y", -1, 1, 1, 2),
-    ("XF", -1, 5, 2), ("Y", 1, 1, 1, 2), ("SQ", 1, 0), ("XF", 1, 5, 1), ("YF", 1, 1, 0, 4), ("SQ", 1, 1), ("X", 1, 6, 2),
-    ("SQ", 1, 2), ("X", -1, 6, 0), ("Y", 1, 1, 0, 7), ("ES", 1), ("SIB", 5, -1), ("Y", -1, 1, 0, 1), ("Y", -1, 1, 1, 3),
-    ("YF", -1, 1, 0, 7), ("SIB", 5, 1), ("YF", 1, 1, 1, 2), ("SIB", 6, 0), ("X", 1, 6, 3), ("SIB", 5, 0), ("X", -1, 6, 1),
-    ("XF", -1, 6, 2), ("XF", -1, 6, 3), ("SIB", 5, 2), ("Y", 1, 1, 1, 3), ("XF", 1, 6, 1), ("ES", 7), ("Y", -1, 1, 1, 4),
-    ("Y", 1, 1, 0, 1), ("XF", 1, 6, 0), ("YF", -1, 1, 0, 1), ("SQ", 5, 0), ("Y", 1, 1, 1, 0), ("SQ", 5, 1), ("SIB", 6, -1),
-    ("SQ", 5, 2), ("YF", 1, 1, 0, 0), ("SIB", 6, 1), ("Y", 1, 1, 0, 5), ("YF", -1, 1, 1, 3), ("ES", 5), ("SIB", 6, 2),
-    ("Y", 1, 1, 1, 1), ("Y", -1, 1, 1, 0), ("Y", -1, 1, 0, 5), ("Y", -1, 1, 1, 1), ("Y", 1, 1, 1, 4), ("SQ", 6, 0),
-    ("SQ", 6, 1), ("SQ", 6, 2), ("Y", -1, 1, 1, 7), ("ES", 6), ("CU", 2, 1), ("Y", 1, 1, 0, 6), ("CU", 1, 0),
-    ("Y", 1, 1, 1, 7), ("CU", 1, 1), ("YF", -1, 1, 0, 5), ("CU", 3, 1), ("Y", -1, 1, 0, 6), ("Y", 1, 1, 1, 5),
-    ("Y", -1, 1, 1, 5), ("CU", 0, 1), ("YF", 1, 1, 0, 6), ("YF", -1, 1, 1, 1), ("CU", 0, 0), ("CU", 0, 2), ("Y", 1, 1, 1, 6),
-    ("CU", 1, 2), ("YF", 1, 1, 1, 0), ("Y", -1, 1, 1, 6), ("CU", 0, 3), ("CU", 2, 0), ("YF", -1, 1, 1, 5), ("YF", 1, 1, 1, 4),
-    ("CU", 1, 3), ("CU", 2, 2), ("YF", -1, 1, 1, 7), ("YF", 1, 1, 1, 6), ("CU", 2, 3), ("CU", 3, 0), ("CU", 3, 2),
-    ("CU", 3, 3),
+    ("ZP", 2), ("X", 1, 7, 0), ("X", -1, 7, 0), ("ZP", 1), ("Z", 2, 0), ("X", -1, 3, 0), ("Y", -1, 0, 0, 6), ("Z", 1, 0),
+    ("ZP", 0), ("Y", -1, 0, 0, 4), ("X", 1, 3, 0), ("Z", 0, 0), ("ZP", 4), ("Z", 4, 0), ("Y", -1, 0, 0, 5), ("Y", 1, 0, 0, 3),
+    ("Y", -1, 0, 0, 1), ("X", -1, 0, 0), ("X", -1, 1, 0), ("X", 1, 2, 0), ("X", -1, 4, 0), ("Y", 1, 0, 0, 6), ("Z", 2, 1),
+    ("Y", 1, 0, 0, 4), ("X", 1, 6, 0), ("X", 1, 0, 0), ("X", -1, 2, 1), ("Y", 1, 0, 0, 7), ("Z", 1, 1), ("X", 1, 1, 0),
+    ("Z", 4, 1), ("Z", 3, 0), ("YF", 1, 0, 0, 4), ("X", -1, 2, 0), ("XF", 1, 2, 0), ("X", 1, 1, 1), ("YF", 1, 0, 0, 6),
+    ("XH", -1, 7), ("Z", 2, 2), ("X", 1, 2, 1), ("X", -1, 2, 2), ("Y", -1, 0, 0, 3), ("Z", 1, 2), ("Z", 0, 1),
+    ("YF", -1, 0, 0, 1), ("X", 1, 4, 1), ("X", -1, 1, 2), ("X", -1, 1, 1), ("Z", 5, 0), ("X", 1, 0, 1), ("Z", 4, 2),
+    ("ZP", 3), ("Z", 2, 3), ("Y", -1, 0, 0, 7), ("XF", 1, 2, 1), ("X", -1, 2, 3), ("Y", 1, 0, 0, 1), ("SIB", 2, 0),
+    ("Z", 1, 3), ("Z", 0, 2), ("XF", -1, 2, 2), ("Y", 1, 0, 1, 2), ("X", 1, 1, 2), ("Y", -1, 0, 1, 2), ("Y", 1, 0, 0, 5),
+    ("Y", -1, 0, 0, 0), ("X", 1, 0, 2), ("Y", 1, 0, 0, 0), ("X", -1, 1, 3), ("X", -1, 4, 2), ("Z", 3, 1), ("Z", 6, 0),
+    ("XF", -1, 2, 3), ("Z", 4, 3), ("XF", 1, 1, 1), ("X", -1, 0, 2), ("SIB", 1, 0), ("Z", 0, 3), ("YF", -1, 0, 0, 7),
+    ("X", 1, 4, 0), ("ZP", 5), ("X", 1, 1, 3), ("X", -1, 4, 3), ("XH", 1, 7), ("Y", -1, 0, 1, 4), ("YF", -1, 0, 0, 5),
+    ("Y", -1, 0, 1, 1), ("X", 1, 2, 3), ("Z", 3, 2), ("Y", 1, 0, 1, 1), ("Z", 3, 3), ("XF", -1, 1, 2), ("Y", 1, 0, 1, 4),
+    ("XF", -1, 1, 3), ("ZP", 6), ("X", 1, 0, 3), ("XF", 1, 1, 0), ("Y", 1, 0, 0, 2), ("X", 1, 2, 2), ("Z", 7, 0),
+    ("X", -1, 0, 3), ("X", 1, 3, 1), ("XF", 1, 0, 1), ("SIB", 2, 1), ("Z", 5, 1), ("Y", -1, 0, 0, 2), ("X", -1, 0, 1),
+    ("YF", 1, 0, 0, 0), ("Z", 6, 1), ("Z", 5, 2), ("ZP", 7), ("Y", -1, 0, 1, 3), ("Y", 1, 0, 1, 0), ("SIB", 1, 1),
+    ("X", -1, 3, 3), ("YF", -1, 0, 1, 1), ("Y", 1, 0, 1, 3), ("YF", 1, 0, 0, 2), ("X", 1, 4, 2), ("YF", -1, 0, 0, 3),
+    ("Y", -1, 0, 1, 0), ("Z", 5, 3), ("XF", -1, 0, 2), ("XF", 1, 0, 0), ("SIB", 0, 0), ("SIB", 2, 2), ("X", 1, 4, 3),
+    ("XF", 1, 4, 0), ("XF", -1, 4, 3), ("Z", 7, 1), ("Z", 6, 2), ("YF", 1, 0, 1, 4), ("XF", -1, 0, 3), ("XF", 1, 4, 1),
+    ("X", 1, 3, 2), ("Z", 7, 2), ("ZT", -1, 7, 0), ("SIB", 3, 0), ("YF", -1, 0, 1, 3), ("X", 1, 6, 1), ("Z", 6, 3),
+    ("YF", 1, 0, 1, 0), ("SIB", 6, 0), ("X", -1, 4, 1), ("X", -1, 3, 2), ("XF", -1, 4, 2), ("SIB", 0, -1), ("Z", 7, 3),
+    ("Y", -1, 0, 1, 5), ("ZT", 1, 7, 0), ("Y", 1, 0, 1, 5), ("ZT", 2, 7, 0), ("X", 1, 3, 3), ("SIB", 7, 0), ("X", -1, 6, 2),
+    ("XF", 1, 3, 1), ("SIB", 0, 1), ("XF", 1, 3, 0), ("XF", -1, 3, 3), ("SIB", 2, -1), ("SIB", 1, -1), ("Y", -1, 0, 1, 6),
+    ("Y", 1, 0, 1, 6), ("SIB", 1, 2), ("Y", -1, 0, 1, 7), ("Y", 1, 0, 1, 7), ("YF", -1, 0, 1, 5), ("SQ", 2, 0),
+    ("ZT", -1, 7, 1), ("YF", 1, 0, 1, 2), ("X", -1, 6, 3), ("X", -1, 3, 1), ("SQ", 1, 0), ("SIB", 0, 2), ("SIB", 4, 1),
+    ("ZT", 1, 7, 1), ("X", 1, 6, 3), ("YF", 1, 0, 1, 6), ("SIB", 4, 0), ("YF", -1, 0, 1, 7), ("SIB", 4, -1), ("SQ", 2, 1),
+    ("XF", -1, 3, 2), ("ZT", 2, 7, 1), ("SQ", 1, 1), ("X", -1, 6, 0), ("ZT", -1, 7, 2), ("X", -1, 6, 1), ("SQ", 0, 0),
+    ("SIB", 4, 2), ("SQ", 0, 1), ("ZT", 1, 7, 2), ("SQ", 0, 2), ("Y", 1, 1, 0, 0), ("Y", -1, 1, 0, 0), ("SQ", 1, 2),
+    ("ZT", -1, 7, 3), ("SIB", 7, -1), ("ZT", 2, 7, 2), ("SQ", 2, 2), ("ES", 0), ("Y", 1, 1, 0, 2), ("X", 1, 6, 2),
+    ("Y", 1, 1, 0, 1), ("ES", 1), ("Y", -1, 1, 0, 1), ("XF", 1, 6, 1), ("ZT", 1, 7, 3), ("Y", -1, 1, 0, 2), ("SIB", 7, 1),
+    ("SQ", 4, 0), ("ZT", 2, 7, 3), ("SIB", 7, 2), ("SQ", 4, 1), ("SQ", 4, 2), ("SIB", 3, -1), ("SIB", 3, 1), ("XF", -1, 6, 2),
+    ("XF", -1, 6, 3), ("YF", 1, 1, 0, 0), ("Y", -1, 1, 0, 4), ("X", -1, 5, 2), ("XF", 1, 6, 0), ("X", 1, 5, 1),
+    ("X", 1, 5, 0), ("ES", 2), ("SIB", 3, 2), ("Y", 1, 1, 0, 4), ("SQ", 7, 0), ("YF", -1, 1, 0, 1), ("SQ", 7, 1),
+    ("SQ", 7, 2), ("YF", 1, 1, 0, 2), ("Y", 1, 1, 0, 7), ("Y", -1, 1, 0, 7), ("X", -1, 5, 3), ("SQ", 3, 0),
+    ("Y", -1, 1, 1, 0), ("SIB", 6, 1), ("SQ", 3, 1), ("SIB", 6, -1), ("SQ", 3, 2), ("ES", 3), ("SIB", 6, 2), ("ES", 7),
+    ("X", -1, 5, 1), ("Y", -1, 1, 0, 3), ("X", 1, 5, 2), ("Y", 1, 1, 0, 3), ("Y", 1, 1, 1, 0), ("XF", 1, 5, 1),
+    ("YF", -1, 1, 0, 7), ("Y", -1, 1, 1, 1), ("X", -1, 5, 0), ("X", 1, 5, 3), ("XF", -1, 5, 2), ("YF", 1, 1, 0, 4),
+    ("SQ", 6, 0), ("SIB", 5, 0), ("SQ", 6, 1), ("SQ", 6, 2), ("XF", -1, 5, 3), ("Y", 1, 1, 0, 6), ("ES", 6), ("XF", 1, 5, 0),
+    ("YF", -1, 1, 0, 3), ("Y", -1, 1, 1, 2), ("ES", 4), ("Y", 1, 1, 1, 2), ("SIB", 5, 1), ("SIB", 5, -1), ("Y", 1, 1, 1, 1),
+    ("YF", -1, 1, 1, 1), ("Y", -1, 1, 1, 3), ("SIB", 5, 2), ("Y", 1, 1, 1, 7), ("Y", -1, 1, 1, 7), ("Y", -1, 1, 0, 6),
+    ("Y", 1, 1, 1, 3), ("YF", 1, 1, 0, 6), ("YF", 1, 1, 1, 0), ("SQ", 5, 0), ("SQ", 5, 1), ("SQ", 5, 2), ("ES", 5),
+    ("Y", -1, 1, 1, 6), ("Y", 1, 1, 1, 6), ("CU", 1, 1), ("Y", 1, 1, 0, 5), ("CU", 2, 0), ("CU", 1, 0), ("Y", -1, 1, 1, 4),
+    ("CU", 2, 1), ("Y", 1, 1, 1, 4), ("Y", -1, 1, 0, 5), ("CU", 0, 1), ("CU", 0, 3), ("Y", -1, 1, 1, 5), ("CU", 3, 0),
+    ("Y", 1, 1, 1, 5), ("CU", 2, 3), ("YF", -1, 1, 1, 7), ("YF", 1, 1, 1, 6), ("CU", 1, 3), ("YF", -1, 1, 0, 5), ("CU", 0, 0),
+    ("YF", 1, 1, 1, 4), ("YF", -1, 1, 1, 5), ("YF", 1, 1, 1, 2), ("CU", 0, 2), ("YF", -1, 1, 1, 3), ("CU", 2, 2),
+    ("CU", 3, 3), ("CU", 1, 2), ("CU", 3, 2), ("CU", 3, 1),
 )
 
 
@@ -70,7 +70,8 @@
     def __init__(self, refs):
         (self.order_in, self.occupancy_in, self.square_in, self.cube_in, self.p_in, self.out, self.order, self.occupancy,
          self.square_pattern, self.cube_pattern, self.panel, self.p_cols, self.s_cols, self.square, self.cube, self.in_sem,
-         self.send_sem, self.z_recv, self.x_recv, self.y_recv, self.sib_recv) = refs
+         self.send_sem, self.z_recv, self.x_recv, self.far_recv, self.exchange_recv, self.pass_recv, self.y_recv,
+         self.sib_recv) = refs
         self.y, self.zh, self.zl, self.x, self.core = (lax.axis_index(name) for name in AXES)
         self.step = self.panel.shape[2] // CHUNKS
         self.waited = set()
@@ -159,52 +160,82 @@
             self.sends_done(8, 15 * first, step, middle)
 
     def x_arrived(self, g, j, o):
-        self.arrived(("x", g, j, o), self.panel_at(g, self.places[o], j), self.x_recv.at[g % 4 - 1, j, o])
+        self.arrived(("x", g, j, o), self.panel_at(g, self.places[o], j), self.x_sem(g, j, o))
+
+    def x_sem(self, g, j, o):
+        alone = o < 2 if g == -1 else o >= 2
+        return self.x_recv.at[(g + 1) // 2, j, o % 2 if alone or j in X_FIRST else 2]
 
     def half_arrived(self, j, sign):
-        self.arrived(("h", j, sign), self.half_at(2, j, sign), self.x_recv.at[1, j, (1 - sign) // 2])
+        self.arrived(("h", j, sign), self.half_at(2, j, sign), self.far_recv.at[j, (1 - sign) // 2])
 
     def group_arrived(self, g, j):
-        if j not in X_FIRST:
-            for o in range(4):
+        if j not in X_FIRST and g == 2:
+            tiles = self.panel.at[self.core, pl.ds(mod4(self.x + 2) * 4, 4), self.rows(j)]
+            self.arrived(("g", j), tiles, self.far_recv.at[j, 0])
+        elif j not in X_FIRST:
+            for o in ((0, 1) if g == -1 else (2, 3)):
                 self.x_arrived(g, j, o)
+            pair = self.panel.at[self.core, pl.ds(0, 2), self.rows(j)]
+            self.arrived(("p", g, j), pair, self.x_recv.at[(g + 1) // 2, j, 2])
         elif g == 2:
             self.half_arrived(j, 1)
             self.half_arrived(j, -1)
         else:
             self.x_arrived(g, j, 0)
 
+    def passed_on(self, d, j):
+        return d == (-1 if j % 2 == 0 else 1)
+
+    def y_sem(self, phase, h, d, j):
+        if d == 0:
+            return self.exchange_recv.at[phase, j]
+        if self.passed_on(d, j):
+            return self.pass_recv.at[phase, h, j]
+        return self.y_recv.at[h, int(d == 2), 0 if phase == 0 else 1 + j // SPAN]
+
     def y_arrived(self, phase, h, d, j):
-        self.arrived(("y", phase, h, d, j), self.cols_at(phase, h, d, j), self.y_recv.at[phase, h, d % 4, j])
+        if d == 0 or self.passed_on(d, j):
+            self.arrived(("y", phase, h, d, j), self.cols_at(phase, h, d, j), self.y_sem(phase, h, d, j))
+        elif phase == 0:
+            self.arrived(("late", 0, h, d == 2), self.p_cols.at[self.group(h, d)], self.y_sem(0, h, d, j))
+        else:
+            span = pl.ds(j // SPAN * 256, 256)
+            self.arrived(("late", 1, h, d == 2, j // SPAN), self.s_cols.at[self.group(h, d), span], self.y_sem(1, h, d, j))
 
     def line(self, g, j, d, kind, at):
         zl = self.zl
         low = self.panel_at(g, lax.max(zl - d, 0), j)
         high = self.panel_at(g, lax.min(zl + d, 3), j)
-        if d > 0:
-            self.arrived(("z", g, j, d, 0), low, self.z_recv.at[0, at, d - 1], zl >= d)
-            self.arrived(("z", g, j, d, 1), high, self.z_recv.at[1, at, d - 1], zl <= 3 - d)
+        end = (zl == 0) | (zl == 3)
+        if d == 1:
+            both = self.panel.at[self.core, pl.ds(0, 2), self.rows(j)]
+            self.arrived(("z", g, j, 1, 2), both, self.z_recv.at[at, 0], (zl == 1) | (zl == 2))
+        if d in (1, 3):
+            self.arrived(("z", g, j, d), low, self.z_recv.at[at, d - 1], end)
+        elif d == 2:
+            self.arrived(("z", g, j, 2), low, self.z_recv.at[at, 1])
         if d < 3:
-            self.send(low, low, kind, self.z_recv.at[0, at, d], self.at_z(1), (zl >= d) & (zl < 3))
-            self.send(high, high, kind, self.z_recv.at[1, at, d], self.at_z(-1), (zl <= 3 - d) & (zl > 0))
+            self.send(low, low, kind, self.z_recv.at[at, d], self.at_z(1), (zl >= d) & (zl < 3))
+            self.send(high, high, kind, self.z_recv.at[at, d], self.at_z(-1), (zl <= 3 - d) & (zl > 0))
 
     def Z(self, j, d):
         if d == 0:
             tile = self.panel_at(0, self.zl, j)
-            self.send(tile, tile, 2, self.z_recv.at[0, j, 0], self.at_z(1), self.zl < 2)
-            self.send(tile, tile, 2, self.z_recv.at[1, j, 0], self.at_z(-1), self.zl >= 2)
+            self.send(tile, tile, 2, self.z_recv.at[j, 0], self.at_z(1), self.zl < 2)
+            self.send(tile, tile, 2, self.z_recv.at[j, 0], self.at_z(-1), self.zl >= 2)
             return
         self.line(0, j, d, 2, j)
         if d >= 2:
             far = 4 - d
             mine = self.p_cols.at[self.group(0, 0), self.rows(j)]
-            self.send(self.panel_at(0, 3 - d, j), mine, 2, self.y_recv.at[0, 1, 0, j], self.at_z(far), self.zl == 3)
-            self.send(self.panel_at(0, d, j), mine, 2, self.y_recv.at[0, 1, 0, j], self.at_z(-far), self.zl == 0)
+            self.send(self.panel_at(0, 3 - d, j), mine, 2, self.y_sem(0, 1, 0, j), self.at_z(far), self.zl == 3)
+            self.send(self.panel_at(0, d, j), mine, 2, self.y_sem(0, 1, 0, j), self.at_z(-far), self.zl == 0)
 
     def ZP(self, j):
         tile = self.panel_at(0, self.zl, j)
-        self.send(tile, tile, 2, self.z_recv.at[1, j, 0], self.at_z(-1), self.zl == 1)
-        self.send(tile, tile, 2, self.z_recv.at[0, j, 0], self.at_z(1), self.zl == 2)
+        self.send(tile, tile, 2, self.z_recv.at[j, 0], self.at_z(-1), self.zl == 1)
+        self.send(tile, tile, 2, self.z_recv.at[j, 0], self.at_z(1), self.zl == 2)
 
     def ZT(self, g, j, d):
         if d == 0:
@@ -213,43 +244,41 @@
 
     def X(self, sign, j, o):
         tile = self.panel_at(0, self.places[o], j)
-        self.send(tile, tile, 7 if j in X_FIRST else 0, self.x_recv.at[-sign % 4 - 1, j, o], self.at_x(sign))
+        self.send(tile, tile, 7 if j in X_FIRST else 0, self.x_sem(-sign, j, o), self.at_x(sign))
 
     def XF(self, sign, j, o):
         self.x_arrived(-sign, j, o)
         tile = self.panel_at(-sign, self.places[o], j)
-        self.send(tile, tile, 1, self.x_recv.at[1, j, o], self.at_x(sign))
+        self.send(tile, tile, 1, self.far_recv.at[j, 0], self.at_x(sign))
 
     def XH(self, sign, j):
         self.x_arrived(-sign, j, 0)
         tile = self.half_at(-sign, j, sign)
-        self.send(tile, tile, 7, self.x_recv.at[1, j, (1 - sign) // 2], self.at_x(sign))
+        self.send(tile, tile, 7, self.far_recv.at[j, (1 - sign) // 2], self.at_x(sign))
 
     def Y(self, sign, phase, h, j):
         if h == 1:
             self.y_arrived(phase, 1, 0, j)
         tile = self.cols_at(phase, h, 0, j)
-        self.send(tile, tile, 3 + phase, self.y_recv.at[phase, h, -sign % 4, j], self.at_y(sign))
+        self.send(tile, tile, 3 + phase, self.y_sem(phase, h, -sign, j), self.at_y(sign))
 
     def YF(self, sign, phase, h, j):
         self.y_arrived(phase, h, -sign, j)
         tile = self.cols_at(phase, h, -sign, j)
-        self.send(tile, tile, 3 + phase, self.y_recv.at[phase, h, 2, j], self.at_y(sign))
+        self.send(tile, tile, 3 + phase, self.y_sem(phase, h, 2, j), self.at_y(sign))
 
     def ES(self, j):
         tile = self.cols_at(1, 0, 0, j)
-        self.send(tile, tile, 5, self.y_recv.at[1, 1, 0, j], self.at_z(4))
+        self.send(tile, tile, 5, self.y_sem(1, 1, 0, j), self.at_z(4))
 
     def SIB(self, j, g):
         if g != 0:
             self.group_arrived(g, j)
         tiles = self.panel.at[self.core, pl.ds(mod4(self.x + g) * 4, 4), self.rows(j)]
-        self.send(tiles, tiles, 6, self.sib_recv.at[j, g % 4], self.other_core())
+        self.send(tiles, tiles, 6, self.sib_recv.at[j], self.other_core())
 
     def sibling_arrived(self, j):
-        for g in (0, -1, 1, 2):
-            tiles = self.panel.at[1 - self.core, pl.ds(mod4(self.x + g) * 4, 4), self.rows(j)]
-            self.arrived(("s", j, g), tiles, self.sib_recv.at[j, g % 4])
+        self.arrived(("s", j), self.panel.at[1 - self.core, :, self.rows(j)], self.sib_recv.at[j])
 
     def square_terms(self, j, y, zh):
         total = None
@@ -326,7 +355,7 @@
             copy.start()
         barrier = pltpu.get_barrier_semaphore()
         partners = [self.at_x(1), self.at_x(-1), self.at_y(1), self.at_y(-1), self.at_z(1), self.at_z(-1), self.at_z(2),
-                    self.at_z(-2), self.at_z(4), self.other_core()]
+                    self.at_z(-2), self.other_core()]
         for device in partners:
             pl.semaphore_signal(barrier, inc=1, device_id=device, device_id_type=pl.DeviceIdType.MESH)
         for copy in inputs:
@@ -375,10 +404,13 @@
             pltpu.VMEM((rows, cols), jnp.float32),
             sem((5,)),
             sem((9,)),
-            sem((2, lines, 3)),
-            sem((3, CHUNKS, 4)),
-            sem((2, 2, 4, CHUNKS)),
-            sem((CHUNKS, 4)),
+            sem((lines, 3)),
+            sem((2, CHUNKS, 3)),
+            sem((CHUNKS, 2)),
+            sem((2, CHUNKS)),
+            sem((2, 2, CHUNKS)),
+            sem((2, 2, 5)),
+            sem((CHUNKS,)),
         ],
         compiler_params=pltpu.CompilerParams(collective_id=0, has_side_effects=True, vmem_limit_bytes=48 * 2**20),
         cost_estimate=pl.CostEstimate(flops=4 * rows * cols * 8192, bytes_accessed=2**24, transcendentals=0),

time: 109 us -> 104 us (0.954)
  Pallas kernels: 104 us -> 98.3 us
    pallas_call x1, Pallas kernels: 104 us -> 98.3 us  [body(): pl.pallas_call(kernel, out_shape=jax.ShapeDtypeStruct((rows, cols), jnp.f...]
where the time goes in v3:
time: 104 us; the launch traced here: 103 us
  Pallas kernels  98.3 us (95%)
  local copies, waits for them, and re-layouts  4.94 us (5%)
    pallas_call x1, Pallas kernels, body(): pl.pallas_call(kernel, out_shape=jax.ShapeDtypeStruct((rows, cols), jnp.f...  98.3 us
    unnamed x11, local copies, waits for them, and re-layouts  4.94 us

profile of v3, /device:TPU:1, one launch (start us, length us, event | category | flops | bytes accessed | tf_op | source)
XLA Modules:
  0.0 103.3 jit_solution(10918930629138478315)
XLA Ops:
  0.0 0.0 copy-start
  0.0 1.0 %copy-done = bf16[1024,256]{1,0:T(8,128)(2,1)S(1)} copy-done((bf16[1024,256]{1,0:T(8,128)(2,1)S(1)}, bf16[1024,256]{1,0:T(8,128)(2,1)}, u32[]{:S(2)}) %copy-start) | copy-done | bytes 524312
  1.0 0.0 copy-start.1
  1.0 0.8 copy-done.1
  1.8 0.0 copy-start.2
  1.8 0.8 copy-done.2
  2.6 0.0 copy-start.3
  2.6 0.8 copy-done.3
  3.3 0.0 copy-start.4
  3.3 0.7 copy-done.4
  4.0 98.3 %shard_map.55 = f32[1024,256]{1,0:T(8,128)S(1)} custom-call(s32[64]{0:T(128)S(1)} %copy-done.4, s32[64,64]{1,0:T(8,128)S(1)} %copy-done.1, s32[64,64]{1,0:T(8,128)S(1)} %copy-done.2, s32[64,64]{1,0:T(8,128)S(1)} %copy-done.3, bf16[1024,256]{1,0:T(8,128)(2,1)S(1)} %copy-done), custom_call_target="tpu_custom_call" | custom-call | flops 8589934592 | bytes 16777216 | tf_op jit(solution)/shard_map/pallas_call | solution.py:390
  102.3 1.0 copy.7
Async XLA Ops:
  0.0 1.0 %copy-start = (bf16[1024,256]{1,0:T(8,128)(2,1)S(1)}, bf16[1024,256]{1,0:T(8,128)(2,1)}, u32[]{:S(2)}) copy-start(bf16[1024,256]{1,0:T(8,128)(2,1)} %refs_4_.1) | copy-start | bytes 1572868
  1.0 0.8 copy-start.1
  1.8 0.8 copy-start.2
  2.6 0.8 copy-start.3
  3.3 0.7 copy-start.4

commit v4 on v3

--- a/solution.py
+++ b/solution.py
@@ -9,56 +9,58 @@
 
 AXES = ("y", "zh", "zl", "x", "core")
 CHUNKS = 8
-X_FIRST = (7,)
+X_FIRST = (2,)
 SPAN = 2
+LAST = 7
 SOURCES = (((0, 0), (0, -1), (0, 1)), ((1, 0), (0, 2)), ((1, -1), (1, 1)), ((1, 2),))
 ORDER = (
-    ("ZP", 2), ("X", 1, 7, 0), ("X", -1, 7, 0), ("ZP", 1), ("Z", 2, 0), ("X", -1, 3, 0), ("Y", -1, 0, 0, 6), ("Z", 1, 0),
-    ("ZP", 0), ("Y", -1, 0, 0, 4), ("X", 1, 3, 0), ("Z", 0, 0), ("ZP", 4), ("Z", 4, 0), ("Y", -1, 0, 0, 5), ("Y", 1, 0, 0, 3),
-    ("Y", -1, 0, 0, 1), ("X", -1, 0, 0), ("X", -1, 1, 0), ("X", 1, 2, 0), ("X", -1, 4, 0), ("Y", 1, 0, 0, 6), ("Z", 2, 1),
-    ("Y", 1, 0, 0, 4), ("X", 1, 6, 0), ("X", 1, 0, 0), ("X", -1, 2, 1), ("Y", 1, 0, 0, 7), ("Z", 1, 1), ("X", 1, 1, 0),
-    ("Z", 4, 1), ("Z", 3, 0), ("YF", 1, 0, 0, 4), ("X", -1, 2, 0), ("XF", 1, 2, 0), ("X", 1, 1, 1), ("YF", 1, 0, 0, 6),
-    ("XH", -1, 7), ("Z", 2, 2), ("X", 1, 2, 1), ("X", -1, 2, 2), ("Y", -1, 0, 0, 3), ("Z", 1, 2), ("Z", 0, 1),
-    ("YF", -1, 0, 0, 1), ("X", 1, 4, 1), ("X", -1, 1, 2), ("X", -1, 1, 1), ("Z", 5, 0), ("X", 1, 0, 1), ("Z", 4, 2),
-    ("ZP", 3), ("Z", 2, 3), ("Y", -1, 0, 0, 7), ("XF", 1, 2, 1), ("X", -1, 2, 3), ("Y", 1, 0, 0, 1), ("SIB", 2, 0),
-    ("Z", 1, 3), ("Z", 0, 2), ("XF", -1, 2, 2), ("Y", 1, 0, 1, 2), ("X", 1, 1, 2), ("Y", -1, 0, 1, 2), ("Y", 1, 0, 0, 5),
-    ("Y", -1, 0, 0, 0), ("X", 1, 0, 2), ("Y", 1, 0, 0, 0), ("X", -1, 1, 3), ("X", -1, 4, 2), ("Z", 3, 1), ("Z", 6, 0),
-    ("XF", -1, 2, 3), ("Z", 4, 3), ("XF", 1, 1, 1), ("X", -1, 0, 2), ("SIB", 1, 0), ("Z", 0, 3), ("YF", -1, 0, 0, 7),
-    ("X", 1, 4, 0), ("ZP", 5), ("X", 1, 1, 3), ("X", -1, 4, 3), ("XH", 1, 7), ("Y", -1, 0, 1, 4), ("YF", -1, 0, 0, 5),
-    ("Y", -1, 0, 1, 1), ("X", 1, 2, 3), ("Z", 3, 2), ("Y", 1, 0, 1, 1), ("Z", 3, 3), ("XF", -1, 1, 2), ("Y", 1, 0, 1, 4),
-    ("XF", -1, 1, 3), ("ZP", 6), ("X", 1, 0, 3), ("XF", 1, 1, 0), ("Y", 1, 0, 0, 2), ("X", 1, 2, 2), ("Z", 7, 0),
-    ("X", -1, 0, 3), ("X", 1, 3, 1), ("XF", 1, 0, 1), ("SIB", 2, 1), ("Z", 5, 1), ("Y", -1, 0, 0, 2), ("X", -1, 0, 1),
-    ("YF", 1, 0, 0, 0), ("Z", 6, 1), ("Z", 5, 2), ("ZP", 7), ("Y", -1, 0, 1, 3), ("Y", 1, 0, 1, 0), ("SIB", 1, 1),
-    ("X", -1, 3, 3), ("YF", -1, 0, 1, 1), ("Y", 1, 0, 1, 3), ("YF", 1, 0, 0, 2), ("X", 1, 4, 2), ("YF", -1, 0, 0, 3),
-    ("Y", -1, 0, 1, 0), ("Z", 5, 3), ("XF", -1, 0, 2), ("XF", 1, 0, 0), ("SIB", 0, 0), ("SIB", 2, 2), ("X", 1, 4, 3),
-    ("XF", 1, 4, 0), ("XF", -1, 4, 3), ("Z", 7, 1), ("Z", 6, 2), ("YF", 1, 0, 1, 4), ("XF", -1, 0, 3), ("XF", 1, 4, 1),
-    ("X", 1, 3, 2), ("Z", 7, 2), ("ZT", -1, 7, 0), ("SIB", 3, 0), ("YF", -1, 0, 1, 3), ("X", 1, 6, 1), ("Z", 6, 3),
-    ("YF", 1, 0, 1, 0), ("SIB", 6, 0), ("X", -1, 4, 1), ("X", -1, 3, 2), ("XF", -1, 4, 2), ("SIB", 0, -1), ("Z", 7, 3),
-    ("Y", -1, 0, 1, 5), ("ZT", 1, 7, 0), ("Y", 1, 0, 1, 5), ("ZT", 2, 7, 0), ("X", 1, 3, 3), ("SIB", 7, 0), ("X", -1, 6, 2),
-    ("XF", 1, 3, 1), ("SIB", 0, 1), ("XF", 1, 3, 0), ("XF", -1, 3, 3), ("SIB", 2, -1), ("SIB", 1, -1), ("Y", -1, 0, 1, 6),
-    ("Y", 1, 0, 1, 6), ("SIB", 1, 2), ("Y", -1, 0, 1, 7), ("Y", 1, 0, 1, 7), ("YF", -1, 0, 1, 5), ("SQ", 2, 0),
-    ("ZT", -1, 7, 1), ("YF", 1, 0, 1, 2), ("X", -1, 6, 3), ("X", -1, 3, 1), ("SQ", 1, 0), ("SIB", 0, 2), ("SIB", 4, 1),
-    ("ZT", 1, 7, 1), ("X", 1, 6, 3), ("YF", 1, 0, 1, 6), ("SIB", 4, 0), ("YF", -1, 0, 1, 7), ("SIB", 4, -1), ("SQ", 2, 1),
-    ("XF", -1, 3, 2), ("ZT", 2, 7, 1), ("SQ", 1, 1), ("X", -1, 6, 0), ("ZT", -1, 7, 2), ("X", -1, 6, 1), ("SQ", 0, 0),
-    ("SIB", 4, 2), ("SQ", 0, 1), ("ZT", 1, 7, 2), ("SQ", 0, 2), ("Y", 1, 1, 0, 0), ("Y", -1, 1, 0, 0), ("SQ", 1, 2),
-    ("ZT", -1, 7, 3), ("SIB", 7, -1), ("ZT", 2, 7, 2), ("SQ", 2, 2), ("ES", 0), ("Y", 1, 1, 0, 2), ("X", 1, 6, 2),
-    ("Y", 1, 1, 0, 1), ("ES", 1), ("Y", -1, 1, 0, 1), ("XF", 1, 6, 1), ("ZT", 1, 7, 3), ("Y", -1, 1, 0, 2), ("SIB", 7, 1),
-    ("SQ", 4, 0), ("ZT", 2, 7, 3), ("SIB", 7, 2), ("SQ", 4, 1), ("SQ", 4, 2), ("SIB", 3, -1), ("SIB", 3, 1), ("XF", -1, 6, 2),
-    ("XF", -1, 6, 3), ("YF", 1, 1, 0, 0), ("Y", -1, 1, 0, 4), ("X", -1, 5, 2), ("XF", 1, 6, 0), ("X", 1, 5, 1),
-    ("X", 1, 5, 0), ("ES", 2), ("SIB", 3, 2), ("Y", 1, 1, 0, 4), ("SQ", 7, 0), ("YF", -1, 1, 0, 1), ("SQ", 7, 1),
-    ("SQ", 7, 2), ("YF", 1, 1, 0, 2), ("Y", 1, 1, 0, 7), ("Y", -1, 1, 0, 7), ("X", -1, 5, 3), ("SQ", 3, 0),
-    ("Y", -1, 1, 1, 0), ("SIB", 6, 1), ("SQ", 3, 1), ("SIB", 6, -1), ("SQ", 3, 2), ("ES", 3), ("SIB", 6, 2), ("ES", 7),
-    ("X", -1, 5, 1), ("Y", -1, 1, 0, 3), ("X", 1, 5, 2), ("Y", 1, 1, 0, 3), ("Y", 1, 1, 1, 0), ("XF", 1, 5, 1),
-    ("YF", -1, 1, 0, 7), ("Y", -1, 1, 1, 1), ("X", -1, 5, 0), ("X", 1, 5, 3), ("XF", -1, 5, 2), ("YF", 1, 1, 0, 4),
-    ("SQ", 6, 0), ("SIB", 5, 0), ("SQ", 6, 1), ("SQ", 6, 2), ("XF", -1, 5, 3), ("Y", 1, 1, 0, 6), ("ES", 6), ("XF", 1, 5, 0),
-    ("YF", -1, 1, 0, 3), ("Y", -1, 1, 1, 2), ("ES", 4), ("Y", 1, 1, 1, 2), ("SIB", 5, 1), ("SIB", 5, -1), ("Y", 1, 1, 1, 1),
-    ("YF", -1, 1, 1, 1), ("Y", -1, 1, 1, 3), ("SIB", 5, 2), ("Y", 1, 1, 1, 7), ("Y", -1, 1, 1, 7), ("Y", -1, 1, 0, 6),
-    ("Y", 1, 1, 1, 3), ("YF", 1, 1, 0, 6), ("YF", 1, 1, 1, 0), ("SQ", 5, 0), ("SQ", 5, 1), ("SQ", 5, 2), ("ES", 5),
-    ("Y", -1, 1, 1, 6), ("Y", 1, 1, 1, 6), ("CU", 1, 1), ("Y", 1, 1, 0, 5), ("CU", 2, 0), ("CU", 1, 0), ("Y", -1, 1, 1, 4),
-    ("CU", 2, 1), ("Y", 1, 1, 1, 4), ("Y", -1, 1, 0, 5), ("CU", 0, 1), ("CU", 0, 3), ("Y", -1, 1, 1, 5), ("CU", 3, 0),
-    ("Y", 1, 1, 1, 5), ("CU", 2, 3), ("YF", -1, 1, 1, 7), ("YF", 1, 1, 1, 6), ("CU", 1, 3), ("YF", -1, 1, 0, 5), ("CU", 0, 0),
-    ("YF", 1, 1, 1, 4), ("YF", -1, 1, 1, 5), ("YF", 1, 1, 1, 2), ("CU", 0, 2), ("YF", -1, 1, 1, 3), ("CU", 2, 2),
-    ("CU", 3, 3), ("CU", 1, 2), ("CU", 3, 2), ("CU", 3, 1),
+    ("ZP", 1), ("X", -1, 7, 0), ("X", 1, 0, 0), ("Z", 1, 0), ("Y", 1, 0, 0, 2), ("Y", -1, 0, 0, 5), ("X", 1, 4, 0),
+    ("Y", -1, 0, 0, 6), ("Y", 1, 0, 0, 4), ("ZP", 4), ("X", 1, 1, 0), ("ZP", 0), ("X", -1, 4, 0), ("Z", 0, 0),
+    ("Y", -1, 0, 0, 0), ("X", 1, 7, 0), ("X", -1, 1, 0), ("Y", 1, 0, 0, 3), ("Y", -1, 0, 0, 4), ("Z", 4, 0), ("X", -1, 2, 0),
+    ("X", 1, 2, 0), ("Z", 1, 1), ("Y", 1, 0, 0, 6), ("Y", 1, 0, 0, 0), ("ZW", 1), ("Z", 0, 1), ("Z", 3, 0), ("X", -1, 5, 0),
+    ("ZW", 4), ("X", -1, 0, 0), ("Y", -1, 0, 0, 3), ("X", -1, 1, 1), ("XF", 1, 0, 0), ("Z", 4, 1), ("XF", 1, 1, 0),
+    ("Y", 1, 0, 0, 5), ("Z", 7, 0), ("Z", 1, 2), ("Y", -1, 0, 0, 1), ("Y", -1, 0, 0, 2), ("YF", 1, 0, 0, 6), ("X", 1, 1, 1),
+    ("Y", -1, 0, 0, 7), ("X", -1, 4, 1), ("X", -1, 1, 2), ("Z", 0, 2), ("Y", 1, 0, 0, 1), ("YF", 1, 0, 0, 4), ("Z", 3, 1),
+    ("X", -1, 3, 0), ("X", 1, 1, 2), ("X", 1, 4, 1), ("XF", 1, 4, 0), ("Z", 4, 2), ("Z", 2, 0), ("Z", 1, 3),
+    ("YF", 1, 0, 0, 0), ("Z", 0, 3), ("X", -1, 0, 2), ("Y", -1, 0, 1, 1), ("SIB", 1, 0), ("X", -1, 4, 2), ("X", 1, 4, 2),
+    ("Z", 7, 1), ("Z", 6, 0), ("X", -1, 0, 3), ("ZP", 3), ("X", 1, 6, 0), ("Z", 4, 3), ("X", 1, 4, 3), ("YF", -1, 0, 0, 5),
+    ("X", -1, 4, 3), ("Y", 1, 0, 1, 0), ("YF", -1, 0, 0, 7), ("YF", -1, 0, 0, 1), ("YF", -1, 0, 0, 3), ("Z", 5, 0),
+    ("X", 1, 1, 3), ("ZW", 0), ("X", -1, 1, 3), ("Z", 3, 2), ("Y", 1, 0, 0, 7), ("YF", -1, 0, 1, 1), ("XF", -1, 1, 2),
+    ("Z", 7, 2), ("Y", 1, 0, 1, 4), ("YF", 1, 0, 1, 0), ("Z", 3, 3), ("XH", 1, 2), ("Z", 7, 3), ("Z", 2, 1), ("X", -1, 0, 1),
+    ("XF", 1, 4, 1), ("X", 1, 0, 1), ("X", 1, 0, 3), ("ZW", 3), ("XF", 1, 1, 1), ("Z", 6, 1), ("XH", -1, 2), ("Z", 5, 1),
+    ("X", 1, 0, 2), ("YF", 1, 0, 1, 4), ("Z", 2, 2), ("Y", -1, 0, 1, 3), ("XF", -1, 4, 3), ("Y", 1, 0, 1, 1), ("Z", 6, 2),
+    ("Y", -1, 0, 1, 7), ("YF", 1, 0, 0, 2), ("XF", -1, 1, 3), ("XF", -1, 4, 2), ("Y", 1, 0, 1, 3), ("Y", -1, 0, 1, 0),
+    ("Z", 5, 2), ("XF", 1, 7, 0), ("ZP", 7), ("ZP", 6), ("YF", -1, 0, 1, 3), ("X", 1, 3, 0), ("X", -1, 6, 2), ("Z", 2, 3),
+    ("X", -1, 7, 2), ("ZT", -1, 2, 0), ("Y", -1, 0, 1, 4), ("YF", -1, 0, 1, 7), ("Z", 6, 3), ("Z", 5, 3), ("Y", 1, 0, 1, 2),
+    ("XF", -1, 0, 2), ("SIB", 1, 1), ("ZW", 7), ("X", 1, 7, 1), ("XF", -1, 0, 3), ("ZT", 1, 2, 0), ("XF", 1, 0, 1), ("ZP", 5),
+    ("SIB", 1, -1), ("Y", 1, 0, 1, 6), ("SIB", 4, -1), ("SIB", 7, 0), ("SIB", 1, 2), ("Y", 1, 0, 1, 7), ("ZT", 2, 2, 0),
+    ("SIB", 4, 0), ("Y", -1, 0, 1, 5), ("YF", 1, 0, 1, 2), ("X", -1, 7, 1), ("X", 1, 6, 2), ("SIB", 0, 0), ("Y", 1, 0, 1, 5),
+    ("Y", -1, 0, 1, 6), ("X", -1, 7, 3), ("X", 1, 7, 3), ("SIB", 4, 1), ("X", 1, 6, 3), ("ZP", 2), ("X", 1, 7, 2),
+    ("SIB", 4, 2), ("Y", -1, 0, 1, 2), ("YF", 1, 0, 1, 6), ("ZW", 6), ("X", -1, 6, 1), ("ZT", -1, 2, 1), ("X", 1, 6, 1),
+    ("X", 1, 3, 1), ("SQ", 1, 0), ("YF", -1, 0, 1, 5), ("XF", -1, 7, 2), ("SIB", 3, 0), ("X", -1, 6, 3), ("SIB", 0, 1),
+    ("ZT", 1, 2, 1), ("XF", -1, 6, 2), ("SIB", 0, -1), ("XF", 1, 7, 1), ("SQ", 4, 0), ("SIB", 0, 2), ("SQ", 1, 1),
+    ("SQ", 4, 1), ("SQ", 4, 2), ("SQ", 1, 2), ("XF", -1, 7, 3), ("ES", 1), ("Y", 1, 1, 0, 4), ("XF", 1, 6, 0), ("SQ", 0, 0),
+    ("X", -1, 6, 0), ("SQ", 0, 1), ("SQ", 0, 2), ("SIB", 6, 0), ("ES", 4), ("ZT", 2, 2, 1), ("SIB", 7, -1), ("XF", 1, 6, 1),
+    ("X", 1, 5, 0), ("XF", -1, 6, 3), ("ZW", 2), ("Y", -1, 1, 0, 4), ("Y", 1, 1, 0, 1), ("Y", 1, 1, 0, 0), ("X", -1, 3, 3),
+    ("X", -1, 3, 2), ("X", -1, 3, 1), ("SIB", 7, 1), ("YF", 1, 1, 0, 4), ("SIB", 6, -1), ("ZT", -1, 2, 2), ("X", -1, 5, 3),
+    ("Y", -1, 1, 0, 0), ("X", 1, 3, 2), ("ZT", 1, 2, 2), ("SIB", 7, 2), ("SX", 7, -1), ("Y", -1, 1, 0, 1), ("SX", 7, 0),
+    ("Y", 1, 1, 1, 1), ("X", 1, 3, 3), ("SX", 7, 1), ("X", -1, 5, 2), ("SIB", 6, 1), ("SIB", 6, 2), ("SIB", 2, 0), ("ZW", 5),
+    ("YF", 1, 1, 0, 0), ("SX", 7, 2), ("Y", -1, 1, 1, 1), ("XF", 1, 3, 1), ("Y", -1, 1, 1, 4), ("X", 1, 5, 3),
+    ("ZT", 2, 2, 2), ("Y", -1, 1, 0, 7), ("ES", 7), ("Y", 1, 1, 0, 8), ("ZT", -1, 2, 3), ("Y", 1, 1, 1, 4), ("ES", 0),
+    ("Y", 1, 1, 0, 7), ("X", 1, 5, 1), ("SIB", 2, -1), ("ZT", 1, 2, 3), ("XF", -1, 3, 3), ("YF", -1, 1, 0, 1), ("SIB", 2, 1),
+    ("XF", 1, 3, 0), ("SQ", 6, 0), ("ZT", 2, 2, 3), ("SIB", 2, 2), ("SQ", 6, 1), ("SQ", 6, 2), ("Y", 1, 1, 0, 6),
+    ("XF", -1, 3, 2), ("YF", -1, 1, 1, 1), ("SIB", 3, 1), ("X", 1, 5, 2), ("X", -1, 5, 1), ("ES", 8), ("XF", 1, 5, 0),
+    ("XF", -1, 5, 3), ("ES", 6), ("YF", 1, 1, 0, 8), ("SIB", 3, -1), ("SQ", 2, 0), ("Y", -1, 1, 0, 6), ("YF", 1, 1, 1, 4),
+    ("SQ", 2, 1), ("SQ", 2, 2), ("XF", -1, 5, 2), ("ES", 2), ("Y", -1, 1, 1, 7), ("Y", 1, 1, 0, 2), ("Y", -1, 1, 0, 2),
+    ("XF", 1, 5, 1), ("SIB", 3, 2), ("Y", 1, 1, 1, 0), ("Y", 1, 1, 1, 8), ("YF", -1, 1, 0, 7), ("Y", 1, 1, 1, 7),
+    ("SIB", 5, -1), ("SIB", 5, 1), ("Y", -1, 1, 1, 8), ("SIB", 5, 0), ("SQ", 3, 0), ("Y", -1, 1, 1, 0), ("YF", 1, 1, 0, 6),
+    ("YF", -1, 1, 1, 7), ("SIB", 5, 2), ("SQ", 3, 1), ("SQ", 3, 2), ("Y", -1, 1, 1, 6), ("Y", -1, 1, 0, 3), ("Y", 1, 1, 1, 6),
+    ("Y", 1, 1, 0, 3), ("YF", 1, 1, 1, 8), ("ES", 3), ("YF", 1, 1, 1, 0), ("SQ", 5, 0), ("SQ", 5, 1), ("SQ", 5, 2), ("ES", 5),
+    ("Y", -1, 1, 0, 5), ("Y", -1, 1, 0, 8), ("CU", 1, 0), ("CU", 2, 0), ("Y", 1, 1, 0, 5), ("Y", -1, 1, 1, 2),
+    ("YF", 1, 1, 1, 6), ("CU", 1, 3), ("Y", 1, 1, 1, 2), ("CU", 2, 3), ("YF", -1, 1, 0, 5), ("Y", 1, 1, 1, 3),
+    ("Y", -1, 1, 1, 3), ("YF", 1, 1, 0, 2), ("CU", 3, 0), ("CU", 0, 0), ("CU", 0, 2), ("Y", -1, 1, 1, 5), ("YF", -1, 1, 0, 3),
+    ("Y", 1, 1, 1, 5), ("CU", 3, 3), ("CU", 1, 2), ("YF", 1, 1, 1, 2), ("CU", 0, 3), ("YF", -1, 1, 1, 3), ("CU", 2, 1),
+    ("YF", -1, 1, 1, 5), ("CU", 0, 1), ("CU", 1, 1), ("CU", 2, 2), ("CU", 3, 1), ("CU", 3, 2),
 )
 
 
@@ -95,6 +97,11 @@
     def rows(self, j):
         return pl.ds(j * self.step, self.step)
 
+    def square_rows(self, j):
+        if j not in (LAST, CHUNKS):
+            return self.rows(j)
+        return pl.ds(LAST * self.step + (self.step // 2 if j == CHUNKS else 0), self.step // 2)
+
     def half_rows(self, j, sign):
         return pl.ds(j * self.step + (0 if sign > 0 else self.step // 2), self.step // 2)
 
@@ -108,7 +115,9 @@
         return 2 * mod4(self.y + d) + (self.zh if h == 0 else 1 - self.zh)
 
     def cols_at(self, phase, h, d, j):
-        return (self.p_cols if phase == 0 else self.s_cols).at[self.group(h, d), self.rows(j)]
+        if phase == 0:
+            return self.p_cols.at[self.group(h, d), self.rows(j)]
+        return self.s_cols.at[self.group(h, d), self.square_rows(j)]
 
     def send(self, src, dst, kind, recv_sem, device, guard=None):
         copy = pltpu.make_async_remote_copy(
@@ -187,12 +196,15 @@
     def passed_on(self, d, j):
         return d == (-1 if j % 2 == 0 else 1)
 
+    def span(self, j):
+        return (LAST if j == CHUNKS else j) // SPAN
+
     def y_sem(self, phase, h, d, j):
         if d == 0:
             return self.exchange_recv.at[phase, j]
         if self.passed_on(d, j):
             return self.pass_recv.at[phase, h, j]
-        return self.y_recv.at[h, int(d == 2), 0 if phase == 0 else 1 + j // SPAN]
+        return self.y_recv.at[h, int(d == 2), 0 if phase == 0 else 1 + self.span(j)]
 
     def y_arrived(self, phase, h, d, j):
         if d == 0 or self.passed_on(d, j):
@@ -200,8 +212,9 @@
         elif phase == 0:
             self.arrived(("late", 0, h, d == 2), self.p_cols.at[self.group(h, d)], self.y_sem(0, h, d, j))
         else:
-            span = pl.ds(j // SPAN * 256, 256)
-            self.arrived(("late", 1, h, d == 2, j // SPAN), self.s_cols.at[self.group(h, d), span], self.y_sem(1, h, d, j))
+            span = self.span(j)
+            part = self.s_cols.at[self.group(h, d), pl.ds(span * 256, 256)]
+            self.arrived(("late", 1, h, d == 2, span), part, self.y_sem(1, h, d, j))
 
     def line(self, g, j, d, kind, at):
         zl = self.zl
@@ -211,7 +224,7 @@
         if d == 1:
             both = self.panel.at[self.core, pl.ds(0, 2), self.rows(j)]
             self.arrived(("z", g, j, 1, 2), both, self.z_recv.at[at, 0], (zl == 1) | (zl == 2))
-        if d in (1, 3):
+        if d == 3 or d == 1 and g != 0:
             self.arrived(("z", g, j, d), low, self.z_recv.at[at, d - 1], end)
         elif d == 2:
             self.arrived(("z", g, j, 2), low, self.z_recv.at[at, 1])
@@ -232,6 +245,10 @@
             self.send(self.panel_at(0, 3 - d, j), mine, 2, self.y_sem(0, 1, 0, j), self.at_z(far), self.zl == 3)
             self.send(self.panel_at(0, d, j), mine, 2, self.y_sem(0, 1, 0, j), self.at_z(-far), self.zl == 0)
 
+    def ZW(self, j):
+        end = (self.zl == 0) | (self.zl == 3)
+        self.arrived(("z", 0, j, 1), self.panel_at(0, self.places[1], j), self.z_recv.at[j, 0], end)
+
     def ZP(self, j):
         tile = self.panel_at(0, self.zl, j)
         self.send(tile, tile, 2, self.z_recv.at[j, 0], self.at_z(-1), self.zl == 1)
@@ -275,10 +292,15 @@
         if g != 0:
             self.group_arrived(g, j)
         tiles = self.panel.at[self.core, pl.ds(mod4(self.x + g) * 4, 4), self.rows(j)]
-        self.send(tiles, tiles, 6, self.sib_recv.at[j], self.other_core())
+        self.send(tiles, tiles, 6, self.sib_recv.at[CHUNKS + g % 4 if j == LAST else j],
+                  self.other_core())
 
     def sibling_arrived(self, j):
         self.arrived(("s", j), self.panel.at[1 - self.core, :, self.rows(j)], self.sib_recv.at[j])
+
+    def sibling_group_arrived(self, j, g):
+        tiles = self.panel.at[1 - self.core, pl.ds(mod4(self.x + g) * 4, 4), self.rows(j)]
+        self.arrived(("sg", j, g), tiles, self.sib_recv.at[CHUNKS + g % 4])
 
     def square_terms(self, j, y, zh):
         total = None
@@ -305,17 +327,47 @@
 
         lax.fori_loop(0, count, add, 0)
         if part == 2:
-            mine = self.group(0, 0)
-            for i, q, keep in self.flags(self.square_pattern, j):
-                at = (pl.ds(i * 128, 128), pl.ds(q * 128, 128))
-                block = self.square[at] * keep
-                self.square[at] = block
-                self.s_cols[(mine,) + at] = block.astype(jnp.bfloat16)
-
-    def CU(self, sources, j):
+            self.keep_square(j)
+
+    def SX(self, j, g):
+        for h in (0, 1):
+            for d in (0, -1, 1, 2):
+                for i in range(CHUNKS):
+                    if (h, d) != (0, 0):
+                        self.y_arrived(0, h, d, i)
+        if g != 0:
+            self.group_arrived(g, j)
+        self.sibling_group_arrived(j, g)
+        x = mod4(self.x + g)
+        zh, pair = x // 2, lax.rem(x, 2)
+
+        def add(zl, carry):
+            total = None
+            for core in range(2):
+                left = self.panel[core, x * 4 + zl, self.rows(j), :]
+                right = self.p_cols[2 * zl + zh, pl.ds(pl.multiple_of((2 * pair + core) * 256, 256), 256), :]
+                term = jnp.dot(left, right, preferred_element_type=jnp.float32)
+                total = term if total is None else total + term
+            self.square[self.rows(j), :] += total
+            return carry
+
+        lax.fori_loop(0, 4, add, 0)
+        if g == 2:
+            self.keep_square(j)
+
+    def keep_square(self, j):
+        mine = self.group(0, 0)
+        for i, q, keep in self.flags(self.square_pattern, j):
+            at = (pl.ds(i * 128, 128), pl.ds(q * 128, 128))
+            block = self.square[at] * keep
+            self.square[at] = block
+            self.s_cols[(mine,) + at] = block.astype(jnp.bfloat16)
+
+    def CU(self, sources, j, last=False):
         terms = []
+        parts = list(range(j * SPAN, (j + 1) * SPAN)) + ([CHUNKS] if LAST // SPAN == j else [])
         for h, d in SOURCES[sources]:
-            for i in range(j * SPAN, (j + 1) * SPAN):
+            for i in parts:
                 if (h, d) != (0, 0):
                     self.y_arrived(1, h, d, i)
             terms.append((mod4(self.y + d), self.zh if h == 0 else 1 - self.zh))
@@ -328,21 +380,30 @@
                 right = self.s_cols[2 * y + zh, pl.ds(j * 256, 256), :]
                 term = jnp.dot(left, right, preferred_element_type=jnp.float32)
                 total = term if total is None else total + term
-            self.cube[rows, :] += total
+            if last:
+                total += self.cube[rows, :]
+                for r in range(2):
+                    for q in range(2):
+                        at = (pl.ds(pl.multiple_of(i * 256 + r * 128, 128), 128), pl.ds(q * 128, 128))
+                        block = total[r * 128:(r + 1) * 128, q * 128:(q + 1) * 128]
+                        self.out[at] = 3.0 * self.square[at] - 2.0 * (block * self.flag(self.cube_pattern, 2 * i + r, q))
+            else:
+                self.cube[rows, :] += total
             return carry
 
         lax.fori_loop(0, 4, add, 0)
 
+    def flag(self, pattern, i, q):
+        a = self.order[self.group(0, 0) * 8 + i]
+        b = self.order[((self.zl * 4 + self.x) * 2 + self.core) * 2 + q]
+        kept = pattern[lax.min(a, b), lax.max(a, b)]
+        return jnp.where(kept > 0, jnp.float32(1), jnp.float32(0))
+
     def flags(self, pattern, j):
-        base_row = self.group(0, 0) * 8
-        base_col = ((self.zl * 4 + self.x) * 2 + self.core) * 2
         count = self.step // 128
         for i in range(j * count, (j + 1) * count):
-            a = self.order[base_row + i]
             for q in range(2):
-                b = self.order[base_col + q]
-                kept = pattern[lax.min(a, b), lax.max(a, b)]
-                yield i, q, jnp.where(kept > 0, jnp.float32(1), jnp.float32(0))
+                yield i, q, self.flag(pattern, i, q)
 
     def run(self):
         mine, place = self.group(0, 0), self.x * 4 + self.zl
@@ -369,12 +430,9 @@
         self.square[...] = jnp.zeros_like(self.square)
         self.cube[...] = jnp.zeros_like(self.cube)
         pl.semaphore_wait(barrier, len(partners))
-        for name, *args in ORDER:
+        for name, *args in ORDER[:-1]:
             getattr(self, name)(*args)
-        for j in range(CHUNKS):
-            for i, q, keep in self.flags(self.cube_pattern, j):
-                at = (pl.ds(i * 128, 128), pl.ds(q * 128, 128))
-                self.out[at] = 3.0 * self.square[at] - 2.0 * (self.cube[at] * keep)
+        self.CU(*ORDER[-1][1:], last=True)
         self.all_sends_done()
 
 
@@ -407,10 +465,10 @@
             sem((lines, 3)),
             sem((2, CHUNKS, 3)),
             sem((CHUNKS, 2)),
-            sem((2, CHUNKS)),
-            sem((2, 2, CHUNKS)),
+            sem((2, CHUNKS + 1)),
+            sem((2, 2, CHUNKS + 1)),
             sem((2, 2, 5)),
-            sem((CHUNKS,)),
+            sem((CHUNKS + 4,)),
         ],
         compiler_params=pltpu.CompilerParams(collective_id=0, has_side_effects=True, vmem_limit_bytes=48 * 2**20),
         cost_estimate=pl.CostEstimate(flops=4 * rows * cols * 8192, bytes_accessed=2**24, transcendentals=0),

time: 104 us -> 102 us (0.981)
  Pallas kernels: 98.3 us -> 95.5 us
    pallas_call x1, Pallas kernels: 98.3 us -> 95.5 us  [body(): pl.pallas_call(kernel, out_shape=jax.ShapeDtypeStruct((rows, cols), jnp.f...]
where the time goes in v4:
time: 102 us; the launch traced here: 100 us
  Pallas kernels  95.5 us (94%)
  local copies, waits for them, and re-layouts  4.94 us (5%)
    pallas_call x1, Pallas kernels, body(): pl.pallas_call(kernel, out_shape=jax.ShapeDtypeStruct((rows, cols), jnp.f...  95.5 us
    unnamed x11, local copies, waits for them, and re-layouts  4.94 us

profile of v4, /device:TPU:1, one launch (start us, length us, event | category | flops | bytes accessed | tf_op | source)
XLA Modules:
  0.0 100.5 jit_solution(17964923918900100526)
XLA Ops:
  0.0 0.0 copy-start
  0.0 1.0 %copy-done = bf16[1024,256]{1,0:T(8,128)(2,1)S(1)} copy-done((bf16[1024,256]{1,0:T(8,128)(2,1)S(1)}, bf16[1024,256]{1,0:T(8,128)(2,1)}, u32[]{:S(2)}) %copy-start) | copy-done | bytes 524312
  1.0 0.0 copy-start.1
  1.0 0.8 copy-done.1
  1.8 0.0 copy-start.2
  1.8 0.8 copy-done.2
  2.6 0.0 copy-start.3
  2.6 0.8 copy-done.3
  3.3 0.0 copy-start.4
  3.3 0.7 copy-done.4
  4.0 95.5 %shard_map.55 = f32[1024,256]{1,0:T(8,128)S(1)} custom-call(s32[64]{0:T(128)S(1)} %copy-done.4, s32[64,64]{1,0:T(8,128)S(1)} %copy-done.1, s32[64,64]{1,0:T(8,128)S(1)} %copy-done.2, s32[64,64]{1,0:T(8,128)S(1)} %copy-done.3, bf16[1024,256]{1,0:T(8,128)(2,1)S(1)} %copy-done), custom_call_target="tpu_custom_call" | custom-call | flops 8589934592 | bytes 16777216 | tf_op jit(solution)/shard_map/pallas_call | solution.py:448
  99.5 1.0 copy.7
Async XLA Ops:
  0.0 1.0 %copy-start = (bf16[1024,256]{1,0:T(8,128)(2,1)S(1)}, bf16[1024,256]{1,0:T(8,128)(2,1)}, u32[]{:S(2)}) copy-start(bf16[1024,256]{1,0:T(8,128)(2,1)} %refs_4_.1) | copy-start | bytes 1572868
  1.0 0.8 copy-start.1
  1.8 0.8 copy-start.2
  2.6 0.8 copy-start.3
  3.3 0.7 copy-start.4

commit v5 on v4

--- a/solution.py
+++ b/solution.py
@@ -373,7 +373,7 @@
             terms.append((mod4(self.y + d), self.zh if h == 0 else 1 - self.zh))
 
         def add(i, carry):
-            rows = pl.ds(pl.multiple_of(i * 256, 256), 256)
+            rows = pl.ds(pl.multiple_of(i * 512, 512), 512)
             total = None
             for y, zh in terms:
                 left = self.panel[j % 2, (2 * zh + j // 2) * 4 + y, rows, :]
@@ -382,16 +382,16 @@
                 total = term if total is None else total + term
             if last:
                 total += self.cube[rows, :]
-                for r in range(2):
+                for r in range(4):
                     for q in range(2):
-                        at = (pl.ds(pl.multiple_of(i * 256 + r * 128, 128), 128), pl.ds(q * 128, 128))
+                        at = (pl.ds(pl.multiple_of(i * 512 + r * 128, 128), 128), pl.ds(q * 128, 128))
                         block = total[r * 128:(r + 1) * 128, q * 128:(q + 1) * 128]
-                        self.out[at] = 3.0 * self.square[at] - 2.0 * (block * self.flag(self.cube_pattern, 2 * i + r, q))
+                        self.out[at] = 3.0 * self.square[at] - 2.0 * (block * self.flag(self.cube_pattern, 4 * i + r, q))
             else:
                 self.cube[rows, :] += total
             return carry
 
-        lax.fori_loop(0, 4, add, 0)
+        lax.fori_loop(0, 2, add, 0)
 
     def flag(self, pattern, i, q):
         a = self.order[self.group(0, 0) * 8 + i]

time: 102 us -> 101 us (level)
  no operation moved by 1% of the time
where the time goes in v5:
time: 101 us; the launch traced here: 99.6 us
  Pallas kernels  94.6 us (94%)
  local copies, waits for them, and re-layouts  4.94 us (5%)
    pallas_call x1, Pallas kernels, body(): pl.pallas_call(kernel, out_shape=jax.ShapeDtypeStruct((rows, cols), jnp.f...  94.6 us
    unnamed x11, local copies, waits for them, and re-layouts  4.94 us

profile of v5, /device:TPU:1, one launch (start us, length us, event | category | flops | bytes accessed | tf_op | source)
XLA Modules:
  0.0 99.6 jit_solution(2367370310783013678)
XLA Ops:
  0.0 0.0 copy-start
  0.0 1.0 %copy-done = bf16[1024,256]{1,0:T(8,128)(2,1)S(1)} copy-done((bf16[1024,256]{1,0:T(8,128)(2,1)S(1)}, bf16[1024,256]{1,0:T(8,128)(2,1)}, u32[]{:S(2)}) %copy-start) | copy-done | bytes 524312
  1.0 0.0 copy-start.1
  1.0 0.8 copy-done.1
  1.8 0.0 copy-start.2
  1.8 0.8 copy-done.2
  2.6 0.0 copy-start.3
  2.6 0.8 copy-done.3
  3.3 0.0 copy-start.4
  3.3 0.7 copy-done.4
  4.0 94.6 %shard_map.55 = f32[1024,256]{1,0:T(8,128)S(1)} custom-call(s32[64]{0:T(128)S(1)} %copy-done.4, s32[64,64]{1,0:T(8,128)S(1)} %copy-done.1, s32[64,64]{1,0:T(8,128)S(1)} %copy-done.2, s32[64,64]{1,0:T(8,128)S(1)} %copy-done.3, bf16[1024,256]{1,0:T(8,128)(2,1)S(1)} %copy-done), custom_call_target="tpu_custom_call" | custom-call | flops 8589934592 | bytes 16777216 | tf_op jit(solution)/shard_map/pallas_call | solution.py:448
  98.6 1.0 copy.7
Async XLA Ops:
  0.0 1.0 %copy-start = (bf16[1024,256]{1,0:T(8,128)(2,1)S(1)}, bf16[1024,256]{1,0:T(8,128)(2,1)}, u32[]{:S(2)}) copy-start(bf16[1024,256]{1,0:T(8,128)(2,1)} %refs_4_.1) | copy-start | bytes 1572868
  1.0 0.8 copy-start.1
  1.8 0.8 copy-start.2
  2.6 0.8 copy-start.3
  3.3 0.7 copy-start.4
